TPU v7x, 32 devices: a whole 2x2x4 slice. The times are simulated.
32 devices in a mesh: dp: 16 (over z, y, core), tensor: 2 (over x).
Axes of the slice: x: 2, y: 2, z: 4, core: 2. Of those that a mesh axis runs over, the one named last changes fastest.
Arguments:
- tokens: bfloat16 [8192, 896], P('dp'), may hold values from -6 to 6
- out_grad: bfloat16 [8192, 896], P('dp'), may hold values from -6 to 6
- doc_lengths: int32 [16, 8], P('dp'), may hold values from 0 to 512, as said below
- q_weight: bfloat16 [896, 896], P(None, 'tensor'), may hold values from -0.1875 to 0.1875
- k_weight: bfloat16 [896, 128], P(None, 'tensor'), may hold values from -0.1875 to 0.1875
- v_weight: bfloat16 [896, 128], P(None, 'tensor'), may hold values from -0.1875 to 0.1875
- q_bias: bfloat16 [14, 64], P('tensor'), may hold values from -3 to 3
- k_bias: bfloat16 [2, 64], P('tensor'), may hold values from -3 to 3
- v_bias: bfloat16 [2, 64], P('tensor'), may hold values from -3 to 3
- o_weight: bfloat16 [896, 896], P('tensor'), may hold values from -1 to 1
- attn_gain: bfloat16 [896], replicated, may hold values from 0.099609375 to 1.8984375
- ffn_gain: bfloat16 [896], replicated, may hold values from 0.099609375 to 1.8984375
- gate_weight: bfloat16 [896, 4864], P(None, 'tensor'), may hold values from -0.1875 to 0.1875
- up_weight: bfloat16 [896, 4864], P(None, 'tensor'), may hold values from -0.1875 to 0.1875
- down_weight: bfloat16 [4864, 896], P('tensor'), may hold values from -0.078125 to 0.078125
Outputs:
- layer_out: bfloat16 [8192, 896], P('dp')
- tokens_grad: bfloat16 [8192, 896], P('dp')
- q_weight_grad: float32 [896, 896], P('dp', 'tensor')
- k_weight_grad: float32 [896, 128], P('dp', 'tensor')
- v_weight_grad: float32 [896, 128], P('dp', 'tensor')
- q_bias_grad: float32 [14, 64], P('tensor', 'dp')
- k_bias_grad: float32 [2, 64], P('tensor')
- v_bias_grad: float32 [2, 64], P('tensor', 'dp')
- o_weight_grad: float32 [896, 896], P('tensor', 'dp')
- attn_gain_grad: float32 [896], P('dp')
- ffn_gain_grad: float32 [896], P('dp')
- gate_weight_grad: float32 [896, 4864], P('dp', 'tensor')
- up_weight_grad: float32 [896, 4864], P('dp', 'tensor')
- down_weight_grad: float32 [4864, 896], P('tensor', 'dp')
Inputs may be any that keep to these rules, and one draw needn't show every extreme that they name: `doc_lengths`: each row lists the sequences of one token buffer, zeros after the last; a row's sum is at most 512, every nonzero entry is 200 or more, the first entry is nonzero, and in every draw some buffer holds one sequence of exactly 512 tokens.
All inputs are finite; a program needn't handle non-finite values.
Results may differ from a plain program's by a relative error of at most 0.024.
Values sent between devices are 32-bit elements; how exact they have to be, the bound alone decides.
No kernel may reach another device: no remote copies, remote signals or barrier semaphores. Data moves between devices by JAX's collectives and lax.ppermute only.
A program may use at most 192 MiB of HBM per device.

v0:
```python
import functools
import math

import jax
import jax.numpy as jnp
from jax import lax
from jax.experimental import pallas as pl
from jax.experimental.pallas import tpu as pltpu
from jax.sharding import PartitionSpec as P

HD = 64


norm_eps = 1e-06
rope_base = 1000000.0


def layout(lengths, row_total):
    doc_ends = jnp.cumsum(lengths)
    places = jnp.arange(row_total, dtype=jnp.int32)
    passed = (places[:, None] >= doc_ends[None, :]).astype(jnp.int32)
    begins = jnp.sum(passed * lengths[None, :], axis=1)
    alive = places < doc_ends[-1]
    return (places - begins, alive)


def rotary(positions, width):
    half_width = width // 2
    inv_freq = jnp.exp(
        jnp.arange(half_width, dtype=jnp.float32) * (-2.0 * math.log(rope_base) / width)
    )
    angles = inv_freq[:, None] * positions.astype(jnp.float32)[None, :]
    return (jnp.cos(angles), jnp.sin(angles))


def norm_back(inputs, factor, gain, upstream):
    scaled = upstream * gain
    return factor * scaled - inputs * factor**3 * jnp.mean(scaled * inputs, axis=-1, keepdims=True)


def swap_tensor(rows):
    size = lax.axis_size("tensor")
    return lax.ppermute(rows, "tensor", [(i, i ^ 1) for i in range(size)])


def swap_dp(rows, bit):
    size = lax.axis_size("dp")
    return lax.ppermute(rows, "dp", [(i, i ^ (1 << bit)) for i in range(size)])


def after(value, *others):
    return lax.optimization_barrier((value, *others))[0]


def dest_columns(width, order, fixed=(), extra=0):
    steps = len(order)
    block = width >> (steps + len(fixed))
    whole = block + extra
    count = whole << steps
    own = lax.axis_index("dp")
    places = jnp.arange(count, dtype=jnp.int32)
    spot = places // whole
    flip = jnp.zeros_like(spot)
    for j, bit in enumerate(order):
        flip = flip + (((spot >> (steps - 1 - j)) & 1) << bit)
    within = places % whole
    source = jnp.where(within < block, (own ^ flip) * block + within, -1)
    chosen = (source[:, None] == jnp.arange(width, dtype=jnp.int32)[None, :]).astype(jnp.bfloat16)
    return chosen[: count // 2], chosen[count // 2 :]


def finish(keep, send, order):
    for bit in order[:-1]:
        sent = swap_dp(send, bit)
        half = sent.shape[0] // 2
        send = keep[half:] + sent[half:]
        keep = keep[:half] + sent[:half]
    return keep + swap_dp(send, order[-1])


def close(keep, sent, order):
    return finish(*step_on(keep, sent), order) if order else keep + sent


def step_on(keep, sent):
    half = sent.shape[0] // 2
    return keep[:half] + sent[:half], keep[half:] + sent[half:]


IN_VMEM = pl.BlockSpec(memory_space=pltpu.VMEM)
LIMIT = 16
EXTRA = 8
ROWS = 64
CUTS = 4
ATTN_CUTS = 4


def contract(left, right, left_dim, right_dim):
    return lax.dot_general(
        left, right, (((left_dim,), (right_dim,)), ((), ())), preferred_element_type=jnp.float32
    )


def over(total, size, step):
    count, rest = divmod(total, size)

    def turn(i, carry):
        step(pl.multiple_of(i * size, size), size)
        return carry

    lax.fori_loop(0, count, turn, 0)
    if rest:
        step(count * size, rest)


def call(kernel, name, shapes, *operands, scratch=()):
    return pl.pallas_call(
        kernel,
        in_specs=[IN_VMEM] * len(operands),
        out_specs=[IN_VMEM] * len(shapes),
        out_shape=[jax.ShapeDtypeStruct(shape, dtype) for shape, dtype in shapes],
        compiler_params=pltpu.CompilerParams(vmem_limit_bytes=LIMIT * 2**20),
        cost_estimate=pl.CostEstimate(flops=1000, bytes_accessed=1000, transcendentals=0),
        scratch_shapes=[pltpu.VMEM(shape, dtype) for shape, dtype in scratch],
        name=name,
    )(*operands)


def turn(pairs, cosine, sine_table):
    half = pairs.shape[0] // 2
    front, back = pairs[:half], pairs[half:]
    return jnp.concatenate([front * cosine - back * sine_table, back * cosine + front * sine_table], axis=0)


def blocks_of(begins_ref, row_total):
    size = row_total // 2
    for first in range(0, row_total, size):
        keys = first + size
        key_place = lax.broadcasted_iota(jnp.int32, (keys, size), 0)
        query_place = lax.broadcasted_iota(jnp.int32, (keys, size), 1) + first
        allowed = (key_place >= begins_ref[:, first:keys]) & (key_place <= query_place)
        yield slice(first, keys), keys, allowed


def attend_kernel(
    heads,
    tokens_ref,
    gain_ref,
    weight_ref,
    bias_ref,
    cosine_ref,
    sine_ref,
    begins_ref,
    normed_ref,
    turned_ref,
    mixed_ref,
    mixed_wide_ref,
    top_ref,
    mass_ref,
    pre_ref,
    mixed_across_ref,
):

    def norm(start):
        rows = pl.ds(start, ROWS)
        inputs = tokens_ref[rows, :].astype(jnp.float32)
        factor = lax.rsqrt(jnp.mean(inputs * inputs, axis=-1, keepdims=True) + norm_eps)
        normed_ref[rows, :] = (inputs * factor * gain_ref[...]).astype(jnp.bfloat16)

    row_blocks(tokens_ref.shape[0], norm)
    pre_ref[...] = contract(weight_ref[...], normed_ref[...], 1, 1) + bias_ref[...]
    cosine, sine_table = cosine_ref[...], sine_ref[...]

    def rope(h, carry):
        r = pl.ds(pl.multiple_of(h * HD, HD), HD)
        turned_ref[r, :] = turn(pre_ref[r, :], cosine, sine_table).astype(jnp.bfloat16)
        return carry

    lax.fori_loop(0, heads + 1, rope, 0)
    value_rows = pre_ref[(heads + 1) * HD :, :].astype(jnp.bfloat16)
    turned_ref[(heads + 1) * HD :, :] = value_rows
    key_rows = turned_ref[heads * HD : (heads + 1) * HD, :].astype(jnp.float32).T.astype(jnp.bfloat16)
    blocks = list(blocks_of(begins_ref, tokens_ref.shape[0]))

    def head(h, carry):
        r = pl.ds(pl.multiple_of(h * HD, HD), HD)
        for cols, keys, allowed in blocks:
            scores = contract(key_rows[:keys], turned_ref[r, cols], 1, 0) * HD ** (-0.5)
            scores = jnp.where(allowed, scores, -1e30)
            top = jnp.max(scores, axis=0, keepdims=True)
            exp_scores = jnp.exp(scores - top)
            mass = 1.0 / jnp.sum(exp_scores, axis=0, keepdims=True)
            low_probs = (exp_scores * mass).astype(jnp.bfloat16)
            mixed_across_ref[r, cols] = contract(value_rows[:, :keys], low_probs, 1, 0)
            top_ref[pl.ds(h, 1), cols] = top
            mass_ref[pl.ds(h, 1), cols] = mass
        return carry

    lax.fori_loop(0, heads, head, 0)
    mixed_wide_ref[...] = mixed_across_ref[: heads * HD, :].astype(jnp.bfloat16).astype(jnp.float32)
    mixed_ref[...] = mixed_across_ref[...].T[:, : heads * HD].astype(jnp.bfloat16)


def project_kernel(
    first_ref,
    tokens_ref,
    mixed_ref,
    other_ref,
    o_ref,
    same_ref,
    cross_ref,
    gain_ref,
    residual_ref,
    two_ref,
    low_ref,
    high_ref,
    o_other_ref,
):
    first = first_ref[...] == 0.0
    o_half = same_ref.shape[0]
    same, cross = same_ref[...], cross_ref[...]
    o_other_ref[:o_half, :] = jnp.where(first, same, cross).astype(jnp.bfloat16)
    o_other_ref[o_half:, :] = jnp.where(first, cross, same).astype(jnp.bfloat16)
    half = low_ref.shape[0]
    for rows, wide_ref in ((slice(0, half), low_ref), (slice(half, 2 * half), high_ref)):
        other = other_ref[:, rows].T.astype(jnp.bfloat16)
        residual = tokens_ref[rows, :].astype(jnp.float32) + (
            contract(mixed_ref[rows, :], o_ref[...], 1, 0) + contract(other, o_other_ref[...], 1, 0)
        )
        residual_ref[rows, :] = residual
        factor = lax.rsqrt(jnp.mean(residual * residual, axis=-1, keepdims=True) + norm_eps)
        two = (residual * factor * gain_ref[...]).astype(jnp.bfloat16)
        two_ref[rows, :] = two
        wide_ref[...] = two.astype(jnp.float32)


def row_blocks(count, step):
    def turn_on(i, carry):
        step(pl.multiple_of(i * ROWS, ROWS))
        return carry

    lax.fori_loop(0, count // ROWS, turn_on, 0)


def norm_back_kernel(*refs):
    part_refs, x_refs = refs[:2], refs[2:4]
    residual_ref, gain_ref, branch_ref, grad_ref, grad_low_ref, gain_grad_ref = refs[4:]
    gain_grad_ref[...] = jnp.zeros(gain_grad_ref.shape, jnp.float32)
    first = 0
    for part_ref, x_ref in zip(part_refs, x_refs):

        def step(start, part_ref=part_ref, x_ref=x_ref, first=first):
            here, rows = pl.ds(start, ROWS), pl.ds(first + start, ROWS)
            residual = residual_ref[rows, :]
            upstream = part_ref[here, :] + x_ref[here, :]
            factor = lax.rsqrt(jnp.mean(residual * residual, axis=-1, keepdims=True) + norm_eps)
            gain_grad_ref[...] += jnp.sum(upstream * (residual * factor), axis=0, keepdims=True)
            grad = norm_back(residual, factor, gain_ref[...], upstream) + branch_ref[rows, :].astype(jnp.float32)
            grad_ref[rows, :] = grad
            grad_low_ref[rows, :] = grad.astype(jnp.bfloat16)

        row_blocks(part_ref.shape[0], step)
        first += part_ref.shape[0]


def tokens_back_kernel(
    tokens_ref, low_ref, high_ref, low_x_ref, high_x_ref, gain_ref, residual_ref, out_grad_ref, alive_ref, grad_ref
):
    half = low_ref.shape[0]
    for first, part_ref, x_ref in ((0, low_ref, low_x_ref), (half, high_ref, high_x_ref)):

        def step(start, part_ref=part_ref, x_ref=x_ref, first=first):
            here, rows = pl.ds(start, ROWS), pl.ds(first + start, ROWS)
            inputs = tokens_ref[rows, :].astype(jnp.float32)
            factor = lax.rsqrt(jnp.mean(inputs * inputs, axis=-1, keepdims=True) + norm_eps)
            grad = norm_back(inputs, factor, gain_ref[...], part_ref[here, :] + x_ref[here, :])
            upstream = out_grad_ref[rows, :].astype(jnp.float32)
            total = upstream * (1.0 - alive_ref[rows, :]) + residual_ref[rows, :] + grad
            grad_ref[rows, :] = total.astype(jnp.bfloat16)

        row_blocks(half, step)


def attend_back_kernel(
    heads,
    residual_ref,
    o_ref,
    weight_ref,
    turned_ref,
    top_ref,
    mass_ref,
    cosine_ref,
    sine_ref,
    begins_ref,
    tokens_ref,
    rows_ref,
    low_ref,
    high_ref,
    gain_grad_ref,
    mixed_ref,
    across_ref,
    key_ref,
    value_ref,
):
    mixed_ref[...] = contract(o_ref[...], residual_ref[...], 1, 1).astype(jnp.bfloat16)
    cosine, sine_table = cosine_ref[...], -sine_ref[...]
    k, v = heads * HD, (heads + 1) * HD
    keys_across = turned_ref[k:v, :]
    key_rows = keys_across.astype(jnp.float32).T.astype(jnp.bfloat16)
    value_rows = turned_ref[v:, :].astype(jnp.float32).T.astype(jnp.bfloat16)
    blocks = list(blocks_of(begins_ref, residual_ref.shape[0]))
    key_ref[...] = jnp.zeros(key_ref.shape, jnp.float32)
    value_ref[...] = jnp.zeros(value_ref.shape, jnp.float32)

    def head(h, carry):
        r = pl.ds(pl.multiple_of(h * HD, HD), HD)
        for cols, keys, allowed in blocks:
            query, grad = turned_ref[r, cols], mixed_ref[r, cols]
            scores = contract(key_rows[:keys], query, 1, 0) * HD ** (-0.5)
            scores = jnp.where(allowed, scores, -1e30)
            probs = jnp.exp(scores - top_ref[pl.ds(h, 1), cols]) * mass_ref[pl.ds(h, 1), cols]
            prob_grad = contract(value_rows[:keys], grad, 1, 0)
            inner_sum = jnp.sum(probs * prob_grad, axis=0, keepdims=True)
            score_grad = (probs * (prob_grad - inner_sum)).astype(jnp.bfloat16)
            query_grad = contract(keys_across[:, :keys], score_grad, 1, 0) * HD ** (-0.5)
            across_ref[r, cols] = turn(query_grad, cosine[:, cols], sine_table[:, cols])
            key_ref[:keys, :] += contract(score_grad, query, 1, 1)
            value_ref[:keys, :] += contract(probs.astype(jnp.bfloat16), grad, 1, 1)
        return carry

    lax.fori_loop(0, heads, head, 0)
    across_ref[k:v, :] = turn(key_ref[...].T * HD ** (-0.5), cosine, sine_table)
    across_ref[v : v + HD, :] = value_ref[...].T
    rows_ref[...] = across_ref[...].T[:, : v + HD].astype(jnp.bfloat16)

    def step(start, size):
        c = pl.ds(start, size)
        part = contract(rows_ref[...], weight_ref[:, c], 1, 0)
        put((low_ref, high_ref), part, c)
        gain_grad_ref[:, c] = jnp.sum(part * (tokens_ref[:, c].astype(jnp.float32) * factor), axis=0, keepdims=True)

    inputs = tokens_ref[...].astype(jnp.float32)
    factor = lax.rsqrt(jnp.mean(inputs * inputs, axis=-1, keepdims=True) + norm_eps)
    over(low_ref.shape[1], 256, step)


def ffn_kernel(*refs):
    if len(refs) == 12:
        side_ref, mine_ref, other_ref, branch_ref, *refs, two_ref, branch_low_ref = refs
        gate_ref, up_ref, down_ref, hidden_ref, gate_rows_ref, up_rows_ref = refs
        half = mine_ref.shape[0]
        first = side_ref[...] == 0.0
        mine, other = mine_ref[...], other_ref[...]
        two_ref[:half, :] = jnp.where(first, mine, other).astype(jnp.bfloat16)
        two_ref[half:, :] = jnp.where(first, other, mine).astype(jnp.bfloat16)
        branch_low_ref[...] = branch_ref[...].astype(jnp.bfloat16)
        low_refs, branch_ref = (), branch_low_ref
    else:
        two_ref, branch_ref, gate_ref, up_ref, down_ref, hidden_ref, gate_rows_ref, up_rows_ref, *low_refs = refs
    if low_refs:
        for wide_ref, low_ref in zip((two_ref, branch_ref), low_refs):
            low_ref[...] = wide_ref[...].astype(jnp.bfloat16)
        two_ref, branch_ref = low_refs

    def step(start, size):
        c = pl.ds(start, size)
        gate = contract(two_ref[...], gate_ref[:, c], 1, 0)
        up = contract(two_ref[...], up_ref[:, c], 1, 0)
        hidden_grad = contract(branch_ref[...], down_ref[c, :], 1, 1)
        sigmoid_gate = 0.5 * jnp.tanh(0.5 * gate) + 0.5
        silu_gate = gate * sigmoid_gate
        hidden_ref[:, c] = (silu_gate * up).astype(jnp.bfloat16)
        gate_rows_ref[:, c] = (hidden_grad * up * (sigmoid_gate + silu_gate * (1.0 - sigmoid_gate))).astype(jnp.bfloat16)
        up_rows_ref[:, c] = (hidden_grad * silu_gate).astype(jnp.bfloat16)

    over(gate_ref.shape[1], 768, step)


def ffn_rows(rows, branch, *weights):
    wide = ((branch.shape[0], weights[0].shape[1]), jnp.bfloat16)
    low = [(branch.shape, jnp.bfloat16)] * 2 if branch.dtype == jnp.float32 else []
    return call(ffn_kernel, "ffn_rows", [wide] * 3 + low, *rows, branch, *weights)


def back_kernel(first, gate_rows_ref, up_rows_ref, gate_ref, up_ref, *part_refs):
    rows = pl.ds(first, len(part_refs) * part_refs[0].shape[0])

    def step(start, size):
        c = pl.ds(start, size)
        total = contract(gate_rows_ref[rows, :], gate_ref[c, :], 1, 1) + contract(
            up_rows_ref[rows, :], up_ref[c, :], 1, 1
        )
        put(part_refs, total, c)

    over(gate_ref.shape[0], 256, step)


def ffn_back(gate_rows, up_rows, gate_weight, up_weight, first, counts):
    shapes = [((count, gate_weight.shape[0]), jnp.float32) for count in counts]
    kernel = functools.partial(back_kernel, first)
    return call(kernel, "ffn_back", shapes, gate_rows, up_rows, gate_weight, up_weight)


def down_kernel(hidden_ref, down_ref, low_ref, high_ref):
    def step(start, size):
        c = pl.ds(start, size)
        put((low_ref, high_ref), contract(hidden_ref[...], down_ref[:, c], 1, 0), c)

    over(down_ref.shape[1], 256, step)


def ffn_down(hidden, down_weight):
    shape = ((hidden.shape[0] // 2, down_weight.shape[1]), jnp.float32)
    return call(down_kernel, "ffn_down", [shape] * 2, hidden, down_weight)


def sums_kernel(pieces, cuts, chosen_ref, *refs):
    rows_refs, feature_refs, refs = refs[:pieces], refs[pieces : 2 * pieces], refs[2 * pieces :]
    picked = [contract(chosen_ref[...], r[...], 1, 1).astype(jnp.bfloat16) for r in rows_refs]

    def step(start, size):
        c = pl.ds(start, size)
        total = sum(contract(p, f[:, c], 1, 0) for p, f in zip(picked, feature_refs))
        if len(refs) == cuts:
            put(refs, total, c)
        else:
            total = total + jnp.concatenate([r[:, c] for r in refs[:cuts]])
            put(refs[cuts:], total, c)

    over(feature_refs[0].shape[1], 640, step)


def put(refs, total, c):
    size = total.shape[0] // len(refs)
    for i, ref in enumerate(refs):
        ref[:, c] = total[i * size : (i + 1) * size]


def outer_sums(chosen, rows, features):
    shape = ((chosen.shape[0] // CUTS, features[0].shape[1]), jnp.float32)
    kernel = functools.partial(sums_kernel, len(rows), CUTS)
    return call(kernel, "outer_sums", [shape] * CUTS, chosen, *rows, *features)


def outer_fold(chosen, rows, features, arrived):
    shape = ((chosen.shape[0] // 2, features[0].shape[1]), jnp.float32)
    kernel = functools.partial(sums_kernel, len(rows), CUTS)
    return call(kernel, "outer_fold", [shape] * 2, chosen, *rows, *features, *arrived)


def swap_cuts(cuts, bit):
    return [swap_dp(cut, bit) for cut in cuts]


def attn_sums_kernel(block, chosen_ref, gains_ref, normed_ref, residual_ref, qkv_ref, mixed_ref, *refs):
    count = chosen_ref.shape[0]
    chosen = chosen_ref[...]
    qkv_width = qkv_ref.shape[1]
    o_start = qkv_width + gains_ref.shape[1]
    ones_row = lax.broadcasted_iota(jnp.int32, (count, normed_ref.shape[0]), 0) % (block + EXTRA) == block
    picked = contract(chosen, normed_ref[...], 1, 1)
    picked = jnp.where(ones_row, 1.0, picked).astype(jnp.bfloat16)
    gains = jnp.dot(
        chosen.astype(jnp.float32), gains_ref[...], preferred_element_type=jnp.float32, precision=lax.Precision.HIGHEST
    )
    picked_residual = contract(chosen, residual_ref[...], 1, 1).astype(jnp.bfloat16)
    total = jnp.concatenate(
        [
            contract(picked, qkv_ref[...], 1, 0),
            gains,
            contract(picked_residual, mixed_ref[...], 1, 0),
            jnp.zeros((count, -mixed_ref.shape[1] % 128), jnp.float32),
        ],
        axis=1,
    )
    if len(refs) == ATTN_CUTS:
        put(refs, total, slice(None))
    else:
        total = total + jnp.concatenate([r[...] for r in refs[:ATTN_CUTS]])
        put(refs[ATTN_CUTS:], total, slice(None))


def attn_sums(block, chosen, gains, normed, residual_low, qkv_rows, mixed, arrived=None):
    count = chosen.shape[0]
    features = qkv_rows.shape[1] + gains.shape[1] + -(-mixed.shape[1] // 128) * 128
    kernel = functools.partial(attn_sums_kernel, block)
    operands = (chosen, gains, normed, residual_low, qkv_rows, mixed)
    if arrived is None:
        return call(kernel, "attn_sums", [((count // ATTN_CUTS, features), jnp.float32)] * ATTN_CUTS, *operands)
    return call(kernel, "attn_fold", [((count // 2, features), jnp.float32)] * 2, *operands, *arrived)


def on_device(
    tokens,
    out_grad,
    doc_lengths,
    q_weight,
    k_weight,
    v_weight,
    q_bias,
    k_bias,
    v_bias,
    o_weight,
    attn_gain,
    ffn_gain,
    gate_weight,
    up_weight,
    down_weight,
):
    row_total, width = tokens.shape
    local_heads = q_weight.shape[1] // HD
    local_kv = k_weight.shape[1] // HD
    dp_size = lax.axis_size("dp")
    dp_bits = dp_size.bit_length() - 1
    pair_bit = 2
    ffn_order = (0, 1) + tuple(range(3, dp_bits))
    attn_order = (0, 1, pair_bit) + tuple(range(3, dp_bits))
    own = lax.axis_index("dp")
    positions, alive = layout(doc_lengths[0], row_total)
    cosine, sine_table = rotary(positions, HD)
    alive_rows = alive.astype(jnp.float32)[:, None]
    places = jnp.arange(row_total, dtype=jnp.int32)
    o_half = o_weight.shape[0] // 2
    o_first = own & 1
    upstream = out_grad.astype(jnp.float32)
    branch_wide = upstream * alive_rows
    o_mine = lax.dynamic_slice_in_dim(o_weight, o_first * o_half, o_half).astype(jnp.float32)
    o_same = swap_tensor(o_mine)
    half_rows = row_total // 2
    pair_branch = swap_dp(branch_wide, pair_bit)
    ffn_keep, ffn_send = dest_columns(width, ffn_order, (pair_bit,))
    attn_keep, attn_send = dest_columns(width, attn_order, extra=EXTRA)
    branch_grad = branch_wide.astype(jnp.bfloat16)
    inputs = tokens.astype(jnp.float32)
    gain_one = attn_gain.astype(jnp.float32)
    gain_two = ffn_gain.astype(jnp.float32)
    qkv_across = jnp.concatenate([q_weight.T, k_weight.T, v_weight.T])
    qkv_bias = jnp.concatenate([q_bias.reshape(-1), k_bias.reshape(-1), v_bias.reshape(-1)]).astype(jnp.float32)
    q_width = local_heads * HD
    k_width = local_kv * HD
    qkv_width = q_width + 2 * k_width
    begins = (places - positions)[None, :]
    padded = -(-qkv_width // 128) * 128
    row_stats = ((-(-local_heads // 8) * 8, row_total), jnp.float32)
    normed, turned, mixed_heads, mixed_wide, top_score, mass = call(
        functools.partial(attend_kernel, local_heads),
        "attend",
        [
            ((row_total, width), jnp.bfloat16),
            ((qkv_width, row_total), jnp.bfloat16),
            ((row_total, q_width), jnp.bfloat16),
            ((q_width, row_total), jnp.float32),
            row_stats,
            row_stats,
        ],
        tokens,
        gain_one[None, :],
        qkv_across,
        qkv_bias[:, None],
        cosine,
        sine_table,
        begins,
        scratch=[((qkv_width, row_total), jnp.float32), ((-(-q_width // 128) * 128, row_total), jnp.float32)],
    )
    mixed_other = swap_tensor(after(mixed_wide, o_same))
    o_same = after(o_same, mixed_heads)
    o_cross = swap_dp(o_same, 0)
    residual, normed_two, low_wide, high_wide = call(
        project_kernel,
        "project",
        [
            ((row_total, width), jnp.float32),
            ((row_total, width), jnp.bfloat16),
            ((half_rows, width), jnp.float32),
            ((half_rows, width), jnp.float32),
        ],
        jnp.broadcast_to(o_first.astype(jnp.float32), (1, width)),
        tokens,
        mixed_heads,
        after(mixed_other, o_cross, ffn_keep, ffn_send, attn_keep, attn_send, branch_grad),
        o_weight,
        o_same,
        o_cross,
        gain_two[None, :],
        scratch=[((q_width, width), jnp.bfloat16)],
    )
    side = jnp.broadcast_to(lax.axis_index("tensor").astype(jnp.float32), (1, width))
    quarter = half_rows // 2
    mine = jnp.where(side == 0.0, low_wide[:quarter], low_wide[quarter:])
    low_mine = swap_dp(mine, pair_bit)
    high_two = swap_dp(high_wide, pair_bit)
    ffn_weights = (gate_weight, up_weight, down_weight)

    hidden_act, gate_grad_rows, up_grad_rows = ffn_rows([normed_two], branch_grad, *ffn_weights)
    backward = (up_grad_rows, gate_weight, up_weight)
    (low_part,) = ffn_back(after(gate_grad_rows, pair_branch, low_mine), *backward, 0, [half_rows])
    low_swapped = swap_tensor(after(low_mine, gate_grad_rows))
    (high_part,) = ffn_back(after(gate_grad_rows, low_part), *backward, half_rows, [half_rows])
    low_from_x = swap_tensor(after(low_part, low_swapped, high_part))
    low_branch, high_branch = pair_branch[:half_rows], pair_branch[half_rows:]
    low_hidden, low_gate, low_up, low_two, low_branch = ffn_rows(
        [side, low_mine, after(low_swapped, high_part)], low_branch, *ffn_weights
    )
    high_from_x = swap_tensor(after(high_part, low_from_x))
    high_hidden, high_gate, high_up, high_two, high_branch = ffn_rows(
        [after(high_two, low_hidden)], high_branch, *ffn_weights
    )
    branch_rows = (branch_grad, low_branch, high_branch)
    two_rows = (normed_two, low_two, high_two)
    down_sums = outer_sums(ffn_send, branch_rows, (hidden_act, low_hidden, high_hidden))
    down_sent = swap_cuts(down_sums, 0)
    low_down, high_down = ffn_down(after(hidden_act, *down_sums), down_weight)
    gate_sums = outer_sums(after(ffn_send, low_from_x, low_down), two_rows, (gate_grad_rows, low_gate, high_gate))
    gate_sent = swap_cuts(gate_sums, 0)
    up_sums = outer_sums(after(ffn_send, *gate_sums), two_rows, (up_grad_rows, low_up, high_up))
    up_sent = swap_cuts(up_sums, 0)
    down_keep, down_send = outer_fold(
        after(ffn_keep, *up_sums), branch_rows, (hidden_act, low_hidden, high_hidden), down_sent
    )
    gate_keep, gate_send = outer_fold(
        after(ffn_keep, down_send), two_rows, (gate_grad_rows, low_gate, high_gate), gate_sent
    )
    up_keep, up_send = outer_fold(after(ffn_keep, gate_send), two_rows, (up_grad_rows, low_up, high_up), up_sent)
    down_from_y, gate_from_y, up_from_y = (swap_dp(v, ffn_order[1]) for v in (down_send, gate_send, up_send))
    wide, low = ((row_total, width), jnp.float32), ((row_total, width), jnp.bfloat16)
    gain_row = ((1, width), jnp.float32)
    residual_grad, residual_low, ffn_gain_sum = call(
        norm_back_kernel,
        "norm_back",
        [wide, low, gain_row],
        low_part,
        high_part,
        low_from_x,
        after(high_from_x, up_send),
        residual,
        gain_two[None, :],
        branch_grad,
    )
    down_keep, down_send = step_on(down_keep, after(down_from_y, residual_low))
    residual_low = after(residual_low, down_send)
    down_from_z = swap_dp(down_send, ffn_order[2])
    half_wide = ((half_rows, width), jnp.float32)
    qkv_grad_rows, low_normed, high_normed, attn_gain_part = call(
        functools.partial(attend_back_kernel, local_heads),
        "attend_back",
        [((row_total, qkv_width), jnp.bfloat16), half_wide, half_wide, gain_row],
        residual_low,
        o_weight,
        qkv_across,
        turned,
        top_score,
        mass,
        cosine,
        sine_table,
        begins,
        tokens,
        scratch=[
            ((q_width, row_total), jnp.bfloat16),
            ((padded, row_total), jnp.float32),
            ((row_total, HD), jnp.float32),
            ((row_total, HD), jnp.float32),
        ],
    )
    gain_sums = jnp.concatenate([attn_gain_part + swap_tensor(attn_gain_part), ffn_gain_sum])
    low_other = swap_tensor(after(low_normed, gain_sums))
    high_other = swap_tensor(after(high_normed, gain_sums))
    gain_columns = jnp.pad(gain_sums, ((0, -qkv_width % 128 - 2), (0, 0))).T
    attn_operands = (gain_columns, normed, residual_low, qkv_grad_rows, mixed_heads)
    gain_block = width // dp_size
    attn_sent = swap_cuts(
        attn_sums(gain_block, after(attn_send, down_from_z), *attn_operands), attn_order[0]
    )
    gate_keep, gate_send = step_on(gate_keep, gate_from_y)
    gate_from_z = swap_dp(gate_send, ffn_order[2])
    attn_part, attn_next = attn_sums(
        gain_block, after(attn_keep, gate_send, low_other), *attn_operands, attn_sent
    )
    attn_from_z = swap_dp(attn_next, attn_order[1])
    low_down_x = swap_tensor(after(low_down, attn_next))
    high_down_x = swap_tensor(after(high_down, attn_next))
    up_keep, up_send = step_on(up_keep, after(up_from_y, attn_next, low_other))
    up_from_z = swap_dp(up_send, ffn_order[2])
    attn_part, attn_next = step_on(attn_part, after(attn_from_z, up_send))
    attn_from_y = swap_dp(attn_next, attn_order[2])
    attn_part, attn_next = step_on(attn_part, after(attn_from_y, gate_from_z))
    attn_from_z = swap_dp(after(attn_next, up_from_z), attn_order[3])
    attn_grad = close(attn_part, attn_from_z, attn_order[4:])
    (tokens_grad,) = call(
        tokens_back_kernel,
        "tokens_back",
        [low],
        tokens,
        low_normed,
        high_normed,
        low_other,
        after(high_other, up_send),
        gain_one[None, :],
        residual_grad,
        out_grad,
        alive_rows,
    )
    high_down_x = after(high_down_x, attn_next)
    block_out = residual + jnp.concatenate([low_down + low_down_x, high_down + high_down_x])
    o_start = -(-qkv_width // 128) * 128
    qkv_grad, o_grad = attn_grad[:gain_block, :qkv_width], attn_grad[:gain_block, o_start : o_start + q_width]
    attn_gain_grad, ffn_gain_grad = attn_grad[:gain_block, qkv_width], attn_grad[:gain_block, qkv_width + 1]
    bias_heads = attn_grad[gain_block, :qkv_width].reshape(local_heads + 2 * local_kv, HD)
    bias_block = HD // dp_size
    bias_own = lax.dynamic_slice_in_dim(bias_heads, own * bias_block, bias_block, axis=1)
    down_grad, gate_grad, up_grad = (
        close(keep, got, ffn_order[3:])
        for keep, got in ((down_keep, down_from_z), (gate_keep, gate_from_z), (up_keep, up_from_z))
    )
    layer_out = jnp.where(alive[:, None], block_out, inputs).astype(jnp.bfloat16)
    return (
        layer_out,
        tokens_grad,
        qkv_grad[:, :q_width],
        qkv_grad[:, q_width : q_width + k_width],
        qkv_grad[:, q_width + k_width :],
        bias_own[:local_heads],
        bias_heads[local_heads : local_heads + local_kv],
        bias_own[local_heads + local_kv :],
        o_grad.T,
        attn_gain_grad,
        ffn_gain_grad,
        gate_grad,
        up_grad,
        down_grad.T,
    )


def solution(mesh):
    return jax.shard_map(
        on_device,
        mesh=mesh,
        in_specs=(
            P("dp", None),
            P("dp", None),
            P("dp", None),
            P(None, "tensor"),
            P(None, "tensor"),
            P(None, "tensor"),
            P("tensor", None),
            P("tensor", None),
            P("tensor", None),
            P("tensor", None),
            P(),
            P(),
            P(None, "tensor"),
            P(None, "tensor"),
            P("tensor", None),
        ),
        out_specs=(
            P("dp", None),
            P("dp", None),
            P("dp", "tensor"),
            P("dp", "tensor"),
            P("dp", "tensor"),
            P("tensor", "dp"),
            P("tensor", None),
            P("tensor", "dp"),
            P("tensor", "dp"),
            P("dp"),
            P("dp"),
            P("dp", "tensor"),
            P("dp", "tensor"),
            P("tensor", "dp"),
        ),
        check_vma=False,
    )
```

profile of v0, /device:TPU:0, one launch (start us, length us, event | category | flops | bytes accessed | tf_op | source)
XLA Modules:
  0.0 258.9 jit_solution(1472411107694386706)
XLA Ops:
  2.7 3.0 %collective-permute-start = (f32[224,896]{1,0:T(8,128)}, f32[224,896]{1,0:T(8,128)}, u32[]{:S(2)}, u32[]{:S(2)}) collective-permute-start(f32[224,896]{1,0:T(8,128)} %dynamic-slice_convert_fusion), channel_id=1, source_target_pairs={{0,1},{1,0},{2,3},{3,2},{4,5},{5,4},{6,7},{7,6},{8,9},{9,8},{10,11... | collective-permute-start | bytes 2408456 | tf_op jit(solution)/shard_map/ppermute | solution.py:43
  13.0 7.6 %attend.1 = (bf16[512,896]{1,0:T(8,128)(2,1)S(1)}, bf16[576,512]{1,0:T(8,128)(2,1)S(1)}, bf16[512,448]{1,0:T(8,128)(2,1)S(1)}, f32[448,512]{1,0:T(8,128)}, f32[8,512]{1,0:T(8,128)S(1)}, /*index=5*/f32[8,512]{1,0:T(8,128)S(1)}) custom-call(bf16[512,896]{1,0:T(8,128)(2,1)S(1)} %copy-done.2, f32[1,896]{1,0:T(1,128)S(1)} %reshape.201.gain_ref, ...), custom_call_target="tpu_custom_call" | custom-call | flops 1000 | bytes 1000 | tf_op jit(solution)/shard_map/attend/pallas_call | solution.py:117
  28.3 17.4 %collective-permute-done.1.other_ref = f32[448,512]{1,0:T(8,128)} collective-permute-done((f32[448,512]{1,0:T(8,128)}, f32[448,512]{1,0:T(8,128)}, u32[]{:S(2)}, u32[]{:S(2)}) %collective-permute-start.1) | collective-permute-done | bytes 917536 | tf_op jit(solution)/shard_map/ppermute | solution.py:43
  45.7 3.4 %project.1 = (f32[512,896]{1,0:T(8,128)S(1)}, bf16[512,896]{1,0:T(8,128)(2,1)S(1)}, f32[256,896]{1,0:T(8,128)S(1)}, f32[256,896]{1,0:T(8,128)S(1)}) custom-call(f32[1,896]{1,0:T(1,128)S(1)} %broadcast_in_dim.30.first_ref, bf16[512,896]{1,0:T(8,128)(2,1)S(1)} %copy-done.2, bf16[512,448]{1,0:T(8,128)(2,1)S(1)} %copy-done.10, ...), custom_call_target="tpu_custom_call" | custom-call | flops 1000 | bytes 1000 | tf_op jit(solution)/shard_map/project/pallas_call | solution.py:117
  53.0 9.1 %ffn_rows.3 = (bf16[512,2432]{1,0:T(8,128)(2,1)S(1)}, bf16[512,2432]{1,0:T(8,128)(2,1)S(1)}, bf16[512,2432]{1,0:T(8,128)(2,1)S(1)}) custom-call(bf16[512,896]{1,0:T(8,128)(2,1)S(1)} %get-tuple-element.107.refs_0_, bf16[512,896]{1,0:T(8,128)(2,1)S(1)} %get-tuple-element.267.refs_1_.refs_0_.refs_6_, bf16[896,2432]{1,0:T(8,128)(2,1)S(1)} %bitcast.17, ...), custom_call_target="tpu_custom_call" | custom-call | flops 1000 | bytes 1000 | tf_op jit(solution)/shard_map/ffn_rows/pallas_call | solution.py:117
  64.1 3.4 %ffn_back.2.refs_0_ = f32[256,896]{1,0:T(8,128)S(1)} custom-call(bf16[512,2432]{1,0:T(8,128)(2,1)S(1)} %get-tuple-element.114.gate_rows_ref.refs_3_, bf16[512,2432]{1,0:T(8,128)(2,1)S(1)} %get-tuple-element.113.up_rows_ref.refs_3_, bf16[896,2432]{1,0:T(8,128)(2,1)S(1)} %bitcast.17, bf16[896,2432]{1,0:T(8,128)(2,1)S(1)} %copy-done), custom_call_target="tpu_custom_call" | custom-call | flops 1000 | bytes 1000 | tf_op jit(solution)/shard_map/ffn_back/pallas_call | solution.py:117
  67.5 3.4 %ffn_back.3.refs_1_ = f32[256,896]{1,0:T(8,128)S(1)} custom-call(bf16[512,2432]{1,0:T(8,128)(2,1)S(1)} %get-tuple-element.114.gate_rows_ref.refs_3_, bf16[512,2432]{1,0:T(8,128)(2,1)S(1)} %get-tuple-element.113.up_rows_ref.refs_3_, bf16[896,2432]{1,0:T(8,128)(2,1)S(1)} %bitcast.17, bf16[896,2432]{1,0:T(8,128)(2,1)S(1)} %copy-done), custom_call_target="tpu_custom_call" | custom-call | flops 1000 | bytes 1000 | tf_op jit(solution)/shard_map/ffn_back/pallas_call | solution.py:117
  75.9 5.0 %ffn_rows.4 = (bf16[256,2432]{1,0:T(8,128)(2,1)S(1)}, bf16[256,2432]{1,0:T(8,128)(2,1)S(1)}, bf16[256,2432]{1,0:T(8,128)(2,1)S(1)}, bf16[256,896]{1,0:T(8,128)(2,1)S(1)}, bf16[256,896]{1,0:T(8,128)(2,1)S(1)}) custom-call(f32[1,896]{1,0:T(1,128)S(1)} %broadcast_in_dim.56.refs_0_, f32[128,896]{1,0:T(8,128)S(1)} %collective-permute-done.3.refs_1_, ...), custom_call_target="tpu_custom_call" | custom-call | flops 1000 | bytes 1000 | tf_op jit(solution)/shard_map/ffn_rows/pallas_call | solution.py:117
  83.5 5.2 %ffn_rows.5 = (bf16[256,2432]{1,0:T(8,128)(2,1)S(1)}, bf16[256,2432]{1,0:T(8,128)(2,1)S(1)}, bf16[256,2432]{1,0:T(8,128)(2,1)S(1)}, bf16[256,896]{1,0:T(8,128)(2,1)S(1)}, bf16[256,896]{1,0:T(8,128)(2,1)S(1)}) custom-call(f32[256,896]{1,0:T(8,128)S(1)} %collective-permute-done.6.refs_0_, f32[256,896]{1,0:T(8,128)S(1)} %get-tuple-element.262.refs_1_, ...), custom_call_target="tpu_custom_call" | custom-call | flops 1000 | bytes 1000 | tf_op jit(solution)/shard_map/ffn_rows/pallas_call | solution.py:117
  92.5 3.4 %ffn_down.1 = (f32[256,896]{1,0:T(8,128)S(1)}, f32[256,896]{1,0:T(8,128)S(1)}) custom-call(bf16[512,2432]{1,0:T(8,128)(2,1)S(1)} %get-tuple-element.126.refs_3_.hidden_ref, bf16[2432,896]{1,0:T(8,128)(2,1)S(1)} %bitcast.19), custom_call_target="tpu_custom_call" | custom-call | flops 1000 | bytes 1000 | tf_op jit(solution)/shard_map/ffn_down/pallas_call | solution.py:117
  95.9 2.8 %outer_sums.4 = (f32[56,2432]{1,0:T(8,128)S(1)}, f32[56,2432]{1,0:T(8,128)S(1)}, f32[56,2432]{1,0:T(8,128)S(1)}, f32[56,2432]{1,0:T(8,128)S(1)}) custom-call(bf16[224,896]{1,0:T(8,128)(2,1)S(1)} %get-tuple-element.138.chosen_ref, bf16[512,896]{1,0:T(8,128)(2,1)S(1)} %get-tuple-element.107.refs_0_, bf16[256,896]{1,0:T(8,128)(2,1)S(1)} %get-tuple-element.130.refs_1_, ...), custom_call_target="tpu_custom_call" | custom-call | flops 1000 | bytes 1000 | tf_op jit(solution)/shard_map/outer_sums/pallas_call | solution.py:117
  108.4 3.8 %outer_fold.4 = (f32[112,2432]{1,0:T(8,128)S(1)}, f32[112,2432]{1,0:T(8,128)}) custom-call(bf16[224,896]{1,0:T(8,128)(2,1)S(1)} %copy-done.7, bf16[512,896]{1,0:T(8,128)(2,1)S(1)} %get-tuple-element.107.refs_0_, bf16[256,896]{1,0:T(8,128)(2,1)S(1)} %get-tuple-element.130.refs_1_, bf16[256,896]{1,0:T(8,128)(2,1)S(1)} %get-tuple-element.131.refs_2_, ...), custom_call_target="tpu_custom_call" | custom-call | flops 1000 | bytes 1000 | tf_op jit(solution)/shard_map/outer_fold/pallas_call | solution.py:117
  116.5 13.1 %collective-permute-done.17.refs_3_ = f32[256,896]{1,0:T(8,128)S(1)} collective-permute-done((f32[256,896]{1,0:T(8,128)S(1)}, f32[256,896]{1,0:T(8,128)S(1)}, u32[]{:S(2)}, u32[]{:S(2)}) %collective-permute-start.17) | collective-permute-done | bytes 917536 | tf_op jit(solution)/shard_map/ppermute | solution.py:43
  137.0 10.4 %attend_back.1 = (bf16[512,576]{1,0:T(8,128)(2,1)S(1)}, f32[256,896]{1,0:T(8,128)S(1)}, f32[256,896]{1,0:T(8,128)S(1)}, f32[1,896]{1,0:T(1,128)S(1)}) custom-call(bf16[512,896]{1,0:T(8,128)(2,1)S(1)} %get-tuple-element.157.residual_ref, bf16[448,896]{1,0:T(8,128)(2,1)S(1)} %copy-done.8, bf16[576,896]{1,0:T(8,128)(2,1)S(1)} %pad_maximum_fusion.weight_ref, ...), custom_call_target="tpu_custom_call" | custom-call | flops 1000 | bytes 1000 | tf_op jit(solution)/shard_map/attend_back/pallas_call | solution.py:117
  155.9 4.9 %collective-permute-done.25 = f32[56,2432]{1,0:T(8,128)} collective-permute-done((f32[56,2432]{1,0:T(8,128)}, f32[56,2432]{1,0:T(8,128)}, u32[]{:S(2)}, u32[]{:S(2)}) %collective-permute-start.25) | collective-permute-done | bytes 544800 | tf_op jit(solution)/shard_map/ppermute | solution.py:48
  164.3 3.4 %attn_sums.1 = (f32[128,1152]{1,0:T(8,128)S(1)}, f32[128,1152]{1,0:T(8,128)S(1)}, f32[128,1152]{1,0:T(8,128)S(1)}, f32[128,1152]{1,0:T(8,128)S(1)}) custom-call(bf16[512,896]{1,0:T(8,128)(2,1)S(1)} %copy-done.21, f32[896,64]{1,0:T(8,128)S(1)} %pad_bitcast_fusion.gains_ref, bf16[512,896]{1,0:T(8,128)(2,1)S(1)} %copy-done.19, bf16[512,896]{1,0:T(8,128)(2,1)S(1)} %copy-done.4, ...), custom_call_target="tpu_custom_call" | custom-call | flops 1000 | bytes 1000 | tf_op jit(solution)/shard_map/attn_sums/pallas_call | solution.py:117
  169.6 5.0 %collective-permute-done.24.low_x_ref = f32[256,896]{1,0:T(8,128)} collective-permute-done((f32[256,896]{1,0:T(8,128)}, f32[256,896]{1,0:T(8,128)}, u32[]{:S(2)}, u32[]{:S(2)}) %collective-permute-start.24) | collective-permute-done | bytes 917536 | tf_op jit(solution)/shard_map/ppermute | solution.py:43
  177.7 3.4 %attn_fold.1 = (f32[256,1152]{1,0:T(8,128)S(1)}, f32[256,1152]{1,0:T(8,128)S(1)}) custom-call(bf16[512,896]{1,0:T(8,128)(2,1)S(1)} %copy-done.20, f32[896,64]{1,0:T(8,128)S(1)} %pad_bitcast_fusion.gains_ref, bf16[512,896]{1,0:T(8,128)(2,1)S(1)} %copy-done.19, bf16[512,896]{1,0:T(8,128)(2,1)S(1)} %copy-done.4, bf16[512,576]{1,0:T(8,128)(2,1)S(1)} %copy-done.23, ...), custom_call_target="tpu_custom_call" | custom-call | flops 1000 | bytes 1000 | tf_op jit(solution)/shard_map/attn_fold/pallas_call | solution.py:117
  181.7 14.7 %collective-permute-done.35 = f32[56,2432]{1,0:T(8,128)S(1)} collective-permute-done((f32[56,2432]{1,0:T(8,128)S(1)}, f32[56,2432]{1,0:T(8,128)S(1)}, u32[]{:S(2)}, u32[]{:S(2)}) %collective-permute-start.35) | collective-permute-done | bytes 544800 | tf_op jit(solution)/shard_map/ppermute | solution.py:48
  201.6 3.7 %tokens_back.1 = bf16[512,896]{1,0:T(8,128)(2,1)} custom-call(bf16[512,896]{1,0:T(8,128)(2,1)S(1)} %copy-done.2, f32[256,896]{1,0:T(8,128)S(1)} %copy-done.33, f32[256,896]{1,0:T(8,128)S(1)} %copy-done.35, f32[256,896]{1,0:T(8,128)} %collective-permute-done.24.low_x_ref, f32[256,896]{1,0:T(8,128)S(1)} %collective-permute-done.36.high_x_ref, ...), custom_call_target="tpu_custom_call" | custom-call | flops 1000 | bytes 1000 | tf_op jit(solution)/shard_map/tokens_back/pallas_call | solution.py:117
  205.3 3.7 %collective-permute-done.32 = f32[256,1152]{1,0:T(8,128)S(1)} collective-permute-done((f32[256,1152]{1,0:T(8,128)S(1)}, f32[256,1152]{1,0:T(8,128)S(1)}, u32[]{:S(2)}, u32[]{:S(2)}) %collective-permute-start.32) | collective-permute-done | bytes 1179680 | tf_op jit(solution)/shard_map/ppermute | solution.py:48
  210.0 16.6 %collective-permute-done.37 = f32[56,2432]{1,0:T(8,128)S(1)} collective-permute-done((f32[56,2432]{1,0:T(8,128)S(1)}, f32[56,2432]{1,0:T(8,128)S(1)}, u32[]{:S(2)}, u32[]{:S(2)}) %collective-permute-start.37) | collective-permute-done | bytes 544800 | tf_op jit(solution)/shard_map/ppermute | solution.py:48
  228.5 11.6 %collective-permute-done.30 = f32[256,896]{1,0:T(8,128)S(1)} collective-permute-done((f32[256,896]{1,0:T(8,128)S(1)}, f32[256,896]{1,0:T(8,128)S(1)}, u32[]{:S(2)}, u32[]{:S(2)}) %collective-permute-start.30) | collective-permute-done | bytes 917536 | tf_op jit(solution)/shard_map/ppermute | solution.py:43
  243.0 11.8 %collective-permute-done.38 = f32[64,1152]{1,0:T(8,128)S(1)} collective-permute-done((f32[64,1152]{1,0:T(8,128)S(1)}, f32[64,1152]{1,0:T(8,128)S(1)}, u32[]{:S(2)}, u32[]{:S(2)}) %collective-permute-start.38) | collective-permute-done | bytes 294944 | tf_op jit(solution)/shard_map/ppermute | solution.py:48
  (246 shorter events, 88.0 us)
Async XLA Ops:
  2.7 21.2 %collective-permute-start = (f32[224,896]{1,0:T(8,128)}, f32[224,896]{1,0:T(8,128)}, u32[]{:S(2)}, u32[]{:S(2)}) collective-permute-start(f32[224,896]{1,0:T(8,128)} %dynamic-slice_convert_fusion), channel_id=1, source_target_pairs={{0,1},{1,0},{2,3},{3,2},{4,5},{5,4},{6,7},{7,6},{8,9},{9,8},{10,11... | collective-permute-start | bytes 2408456 | tf_op jit(solution)/shard_map/ppermute | solution.py:43
  9.4 54.8 %collective-permute-start.5 = (f32[512,896]{1,0:T(8,128)}, f32[512,896]{1,0:T(8,128)}, u32[]{:S(2)}, u32[]{:S(2)}) collective-permute-start(f32[512,896]{1,0:T(8,128)} %get-tuple-element.266), channel_id=1, source_target_pairs={{0,8},{2,10},{4,12},{6,14},{8,0},{10,2},{12,4},{14,6},{16,24},{18,... | collective-permute-start | bytes 5505032 | tf_op jit(solution)/shard_map/ppermute | solution.py:48
  23.9 21.8 %collective-permute-start.1 = (f32[448,512]{1,0:T(8,128)}, f32[448,512]{1,0:T(8,128)}, u32[]{:S(2)}, u32[]{:S(2)}) collective-permute-start(f32[448,512]{1,0:T(8,128)} %get-tuple-element.103), channel_id=1, source_target_pairs={{0,1},{1,0},{2,3},{3,2},{4,5},{5,4},{6,7},{7,6},{8,9},{9,8},{10,11... | collective-permute-start | bytes 2752520 | tf_op jit(solution)/shard_map/ppermute | solution.py:43
  49.2 12.9 %collective-permute-start.3 = (f32[128,896]{1,0:T(8,128)S(1)}, f32[128,896]{1,0:T(8,128)S(1)}, u32[]{:S(2)}, u32[]{:S(2)}) collective-permute-start(f32[128,896]{1,0:T(8,128)S(1)} %slice_select_fusion), channel_id=1, source_target_pairs={{0,8},{2,10},{4,12},{6,14},{8,0},{10,2},{12,4},{14,6},{16,24},{18,... | collective-permute-start | bytes 1376264 | tf_op jit(solution)/shard_map/ppermute | solution.py:48
  62.1 10.7 %collective-permute-start.4 = (f32[128,896]{1,0:T(8,128)S(1)}, f32[128,896]{1,0:T(8,128)S(1)}, u32[]{:S(2)}, u32[]{:S(2)}) collective-permute-start(f32[128,896]{1,0:T(8,128)S(1)} %collective-permute-done.3.refs_1_), channel_id=1, source_target_pairs={{0,1},{1,0},{2,3},{3,2},{4,5},{5,4},{6,7},{7,6},{8,9},{9,8},{10,11... | collective-permute-start | bytes 1376264 | tf_op jit(solution)/shard_map/ppermute | solution.py:43
  63.7 19.8 %collective-permute-start.6 = (f32[256,896]{1,0:T(8,128)S(1)}, f32[256,896]{1,0:T(8,128)S(1)}, u32[]{:S(2)}, u32[]{:S(2)}) collective-permute-start(f32[256,896]{1,0:T(8,128)S(1)} %get-tuple-element.117), channel_id=1, source_target_pairs={{0,8},{2,10},{4,12},{6,14},{8,0},{10,2},{12,4},{14,6},{16,24},{18,... | collective-permute-start | bytes 2752520 | tf_op jit(solution)/shard_map/ppermute | solution.py:48
  72.8 23.1 %collective-permute-start.7 = (f32[256,896]{1,0:T(8,128)S(1)}, f32[256,896]{1,0:T(8,128)}, u32[]{:S(2)}, u32[]{:S(2)}) collective-permute-start(f32[256,896]{1,0:T(8,128)S(1)} %ffn_back.2.refs_0_), channel_id=1, source_target_pairs={{0,1},{1,0},{2,3},{3,2},{4,5},{5,4},{6,7},{7,6},{8,9},{9,8},{10,11... | collective-permute-start | bytes 2752520 | tf_op jit(solution)/shard_map/ppermute | solution.py:43
  91.5 10.6 %collective-permute-start.9 = (f32[56,2432]{1,0:T(8,128)S(1)}, f32[56,2432]{1,0:T(8,128)S(1)}, u32[]{:S(2)}, u32[]{:S(2)}) collective-permute-start(f32[56,2432]{1,0:T(8,128)S(1)} %get-tuple-element.123), channel_id=1, source_target_pairs={{0,2},{2,0},{4,6},{6,4},{8,10},{10,8},{12,14},{14,12},{16,18},{18,... | collective-permute-start | bytes 1634312 | tf_op jit(solution)/shard_map/ppermute | solution.py:48
  92.0 10.3 %collective-permute-start.10 = (f32[56,2432]{1,0:T(8,128)S(1)}, f32[56,2432]{1,0:T(8,128)S(1)}, u32[]{:S(2)}, u32[]{:S(2)}) collective-permute-start(f32[56,2432]{1,0:T(8,128)S(1)} %get-tuple-element.124), channel_id=1, source_target_pairs={{0,2},{2,0},{4,6},{6,4},{8,10},{10,8},{12,14},{14,12},{16,18},{18,... | collective-permute-start | bytes 1634312 | tf_op jit(solution)/shard_map/ppermute | solution.py:48
  92.1 10.7 %collective-permute-start.11 = (f32[56,2432]{1,0:T(8,128)S(1)}, f32[56,2432]{1,0:T(8,128)S(1)}, u32[]{:S(2)}, u32[]{:S(2)}) collective-permute-start(f32[56,2432]{1,0:T(8,128)S(1)} %get-tuple-element.125), channel_id=1, source_target_pairs={{0,2},{2,0},{4,6},{6,4},{8,10},{10,8},{12,14},{14,12},{16,18},{18,... | collective-permute-start | bytes 1634312 | tf_op jit(solution)/shard_map/ppermute | solution.py:48
  105.7 27.9 %collective-permute-start.22 = (f32[112,2432]{1,0:T(8,128)S(1)}, f32[112,2432]{1,0:T(8,128)S(1)}, u32[]{:S(2)}, u32[]{:S(2)}) collective-permute-start(f32[112,2432]{1,0:T(8,128)S(1)} %get-tuple-element.146), channel_id=1, source_target_pairs={{0,4},{2,6},{4,0},{6,2},{8,12},{10,14},{12,8},{14,10},{16,20},{18,... | collective-permute-start | bytes 3268616 | tf_op jit(solution)/shard_map/ppermute | solution.py:48
  107.3 22.4 %collective-permute-start.17 = (f32[256,896]{1,0:T(8,128)S(1)}, f32[256,896]{1,0:T(8,128)S(1)}, u32[]{:S(2)}, u32[]{:S(2)}) collective-permute-start(f32[256,896]{1,0:T(8,128)S(1)} %copy-done.15), channel_id=1, source_target_pairs={{0,1},{1,0},{2,3},{3,2},{4,5},{5,4},{6,7},{7,6},{8,9},{9,8},{10,11... | collective-permute-start | bytes 2752520 | tf_op jit(solution)/shard_map/ppermute | solution.py:43
  113.2 54.5 %collective-permute-start.16 = (f32[112,2432]{1,0:T(8,128)}, f32[112,2432]{1,0:T(8,128)}, u32[]{:S(2)}, u32[]{:S(2)}) collective-permute-start(f32[112,2432]{1,0:T(8,128)} %get-tuple-element.149), channel_id=1, source_target_pairs={{0,4},{2,6},{4,0},{6,2},{8,12},{10,14},{12,8},{14,10},{16,20},{18,... | collective-permute-start | bytes 3268616 | tf_op jit(solution)/shard_map/ppermute | solution.py:48
  134.4 26.4 %collective-permute-start.25 = (f32[56,2432]{1,0:T(8,128)}, f32[56,2432]{1,0:T(8,128)}, u32[]{:S(2)}, u32[]{:S(2)}) collective-permute-start(f32[56,2432]{1,0:T(8,128)} %slice_add_fusion.5), channel_id=1, source_target_pairs={{0,16},{2,18},{4,20},{6,22},{8,24},{10,26},{12,28},{14,30},{16,0},... | collective-permute-start | bytes 1634312 | tf_op jit(solution)/shard_map/ppermute | solution.py:48
  153.8 20.9 %collective-permute-start.24 = (f32[256,896]{1,0:T(8,128)}, f32[256,896]{1,0:T(8,128)}, u32[]{:S(2)}, u32[]{:S(2)}) collective-permute-start(f32[256,896]{1,0:T(8,128)} %copy-done.32), channel_id=1, source_target_pairs={{0,1},{1,0},{2,3},{3,2},{4,5},{5,4},{6,7},{7,6},{8,9},{9,8},{10,11... | collective-permute-start | bytes 2752520 | tf_op jit(solution)/shard_map/ppermute | solution.py:43
  155.0 43.9 %collective-permute-start.33 = (f32[112,2432]{1,0:T(8,128)}, f32[112,2432]{1,0:T(8,128)}, u32[]{:S(2)}, u32[]{:S(2)}) collective-permute-start(f32[112,2432]{1,0:T(8,128)} %copy-done.44), channel_id=1, source_target_pairs={{0,4},{2,6},{4,0},{6,2},{8,12},{10,14},{12,8},{14,10},{16,20},{18,... | collective-permute-start | bytes 3268616 | tf_op jit(solution)/shard_map/ppermute | solution.py:48
  169.0 27.4 %collective-permute-start.35 = (f32[56,2432]{1,0:T(8,128)S(1)}, f32[56,2432]{1,0:T(8,128)S(1)}, u32[]{:S(2)}, u32[]{:S(2)}) collective-permute-start(f32[56,2432]{1,0:T(8,128)S(1)} %slice_add_fusion.3), channel_id=1, source_target_pairs={{0,16},{2,18},{4,20},{6,22},{8,24},{10,26},{12,28},{14,30},{16,0},... | collective-permute-start | bytes 1634312 | tf_op jit(solution)/shard_map/ppermute | solution.py:48
  177.1 24.5 %collective-permute-start.36 = (f32[256,896]{1,0:T(8,128)S(1)}, f32[256,896]{1,0:T(8,128)S(1)}, u32[]{:S(2)}, u32[]{:S(2)}) collective-permute-start(f32[256,896]{1,0:T(8,128)S(1)} %copy-done.35), channel_id=1, source_target_pairs={{0,1},{1,0},{2,3},{3,2},{4,5},{5,4},{6,7},{7,6},{8,9},{9,8},{10,11... | collective-permute-start | bytes 2752520 | tf_op jit(solution)/shard_map/ppermute | solution.py:43
  181.1 27.9 %collective-permute-start.32 = (f32[256,1152]{1,0:T(8,128)S(1)}, f32[256,1152]{1,0:T(8,128)S(1)}, u32[]{:S(2)}, u32[]{:S(2)}) collective-permute-start(f32[256,1152]{1,0:T(8,128)S(1)} %get-tuple-element.173), channel_id=1, source_target_pairs={{0,4},{2,6},{4,0},{6,2},{8,12},{10,14},{12,8},{14,10},{16,20},{18,... | collective-permute-start | bytes 3538952 | tf_op jit(solution)/shard_map/ppermute | solution.py:48
  198.3 42.0 %collective-permute-start.31 = (f32[256,896]{1,0:T(8,128)S(1)}, f32[256,896]{1,0:T(8,128)S(1)}, u32[]{:S(2)}, u32[]{:S(2)}) collective-permute-start(f32[256,896]{1,0:T(8,128)S(1)} %copy-done.37), channel_id=1, source_target_pairs={{0,1},{1,0},{2,3},{3,2},{4,5},{5,4},{6,7},{7,6},{8,9},{9,8},{10,11... | collective-permute-start | bytes 2752520 | tf_op jit(solution)/shard_map/ppermute | solution.py:43
  198.9 41.2 %collective-permute-start.30 = (f32[256,896]{1,0:T(8,128)S(1)}, f32[256,896]{1,0:T(8,128)S(1)}, u32[]{:S(2)}, u32[]{:S(2)}) collective-permute-start(f32[256,896]{1,0:T(8,128)S(1)} %copy-done.39), channel_id=1, source_target_pairs={{0,1},{1,0},{2,3},{3,2},{4,5},{5,4},{6,7},{7,6},{8,9},{9,8},{10,11... | collective-permute-start | bytes 2752520 | tf_op jit(solution)/shard_map/ppermute | solution.py:43
  201.5 25.1 %collective-permute-start.37 = (f32[56,2432]{1,0:T(8,128)S(1)}, f32[56,2432]{1,0:T(8,128)S(1)}, u32[]{:S(2)}, u32[]{:S(2)}) collective-permute-start(f32[56,2432]{1,0:T(8,128)S(1)} %slice_add_fusion.4), channel_id=1, source_target_pairs={{0,16},{2,18},{4,20},{6,22},{8,24},{10,26},{12,28},{14,30},{16,0},... | collective-permute-start | bytes 1634312 | tf_op jit(solution)/shard_map/ppermute | solution.py:48
  209.1 31.1 %collective-permute-start.34 = (f32[128,1152]{1,0:T(8,128)S(1)}, f32[128,1152]{1,0:T(8,128)S(1)}, u32[]{:S(2)}, u32[]{:S(2)}) collective-permute-start(f32[128,1152]{1,0:T(8,128)S(1)} %get-tuple-element.260), channel_id=1, source_target_pairs={{0,8},{2,10},{4,12},{6,14},{8,0},{10,2},{12,4},{14,6},{16,24},{18,... | collective-permute-start | bytes 1769480 | tf_op jit(solution)/shard_map/ppermute | solution.py:48
  240.5 14.3 %collective-permute-start.38 = (f32[64,1152]{1,0:T(8,128)S(1)}, f32[64,1152]{1,0:T(8,128)S(1)}, u32[]{:S(2)}, u32[]{:S(2)}) collective-permute-start(f32[64,1152]{1,0:T(8,128)S(1)} %slice_add_fusion.7), channel_id=1, source_target_pairs={{0,16},{2,18},{4,20},{6,22},{8,24},{10,26},{12,28},{14,30},{16,0},... | collective-permute-start | bytes 884744 | tf_op jit(solution)/shard_map/ppermute | solution.py:48
  (74 other events, 682.3 us)
where the time goes:
time: 260 us; the launch traced here: 259 us
  waiting for transfers between devices  107 us (41%)
  Pallas kernels  81.6 us (31%)
  starting transfers between devices  26.6 us (10%)
  local copies, waits for them, and re-layouts  22.8 us (9%)
  other arithmetic  19.6 us (8%)
    pallas_call x19, Pallas kernels, call(): pl.pallas_call(kernel, in_specs=[IN_VMEM] * len(operands), out_specs=[IN_...  81.6 us
    ppermute x29, waiting for transfers between devices, swap_dp(): return lax.ppermute(rows, 'dp', [(i, i ^ 1 << bit) for i in range(size)])  54.1 us
    ppermute x10, waiting for transfers between devices, swap_tensor(): return lax.ppermute(rows, 'tensor', [(i, i ^ 1) for i in range(size)])  52.7 us
    ppermute x29, starting transfers between devices, swap_dp(): return lax.ppermute(rows, 'dp', [(i, i ^ 1 << bit) for i in range(size)])  14.6 us
    unnamed x119, local copies, waits for them, and re-layouts  14.5 us
    ppermute x10, starting transfers between devices, swap_tensor(): return lax.ppermute(rows, 'tensor', [(i, i ^ 1) for i in range(size)])  12 us
  transfers between devices with their start and end apart: 39, of which 13 were waited for; matrix products, arithmetic and copies ran while one was open for 9% of the time, Pallas kernels for 32%

commit v1 on v0

--- a/solution.py
+++ b/solution.py
@@ -88,7 +88,7 @@
 
 
 IN_VMEM = pl.BlockSpec(memory_space=pltpu.VMEM)
-LIMIT = 16
+LIMIT = 11
 EXTRA = 8
 ROWS = 64
 CUTS = 4

time: 260 us -> 258 us (level)
    unnamed x119 -> x115, local copies, waits for them, and re-layouts: 14.5 us -> 14.6 us
  transfers between devices with their start and end apart: 39 -> 39, of which waited for: 13 -> 14; matrix products, arithmetic and copies ran while one was open for 9% -> 9% of each run, Pallas kernels for 32% -> 31%
where the time goes in v1:
time: 258 us
  waiting for transfers between devices  105 us (41%)
  Pallas kernels  80.2 us (31%)
  starting transfers between devices  28.9 us (11%)
  local copies, waits for them, and re-layouts  22.8 us (9%)
  other arithmetic  19.6 us (8%)
    pallas_call x19, Pallas kernels, call(): pl.pallas_call(kernel, in_specs=[IN_VMEM] * len(operands), out_specs=[IN_...  80.2 us
    ppermute x10, waiting for transfers between devices, swap_tensor(): return lax.ppermute(rows, 'tensor', [(i, i ^ 1) for i in range(size)])  52.7 us
    ppermute x29, waiting for transfers between devices, swap_dp(): return lax.ppermute(rows, 'dp', [(i, i ^ 1 << bit) for i in range(size)])  52.1 us
    ppermute x29, starting transfers between devices, swap_dp(): return lax.ppermute(rows, 'dp', [(i, i ^ 1 << bit) for i in range(size)])  16.9 us
    unnamed x115, local copies, waits for them, and re-layouts  14.6 us
    ppermute x10, starting transfers between devices, swap_tensor(): return lax.ppermute(rows, 'tensor', [(i, i ^ 1) for i in range(size)])  12 us
  transfers between devices with their start and end apart: 39, of which 14 were waited for; matrix products, arithmetic and copies ran while one was open for 9% of the time, Pallas kernels for 31%

profile of v1, /device:TPU:0, one launch (start us, length us, event | category | flops | bytes accessed | tf_op | source)
XLA Modules:
  0.0 257.8 jit_solution(1665400438349995355)
XLA Ops:
  2.7 3.0 %collective-permute-start = (f32[224,896]{1,0:T(8,128)}, f32[224,896]{1,0:T(8,128)}, u32[]{:S(2)}, u32[]{:S(2)}) collective-permute-start(f32[224,896]{1,0:T(8,128)} %dynamic-slice_convert_fusion), channel_id=1, source_target_pairs={{0,1},{1,0},{2,3},{3,2},{4,5},{5,4},{6,7},{7,6},{8,9},{9,8},{10,11... | collective-permute-start | bytes 2408456 | tf_op jit(solution)/shard_map/ppermute | solution.py:43
  13.0 7.6 %attend.1 = (bf16[512,896]{1,0:T(8,128)(2,1)S(1)}, bf16[576,512]{1,0:T(8,128)(2,1)S(1)}, bf16[512,448]{1,0:T(8,128)(2,1)S(1)}, f32[448,512]{1,0:T(8,128)}, f32[8,512]{1,0:T(8,128)S(1)}, /*index=5*/f32[8,512]{1,0:T(8,128)S(1)}) custom-call(bf16[512,896]{1,0:T(8,128)(2,1)S(1)} %copy-done.2, f32[1,896]{1,0:T(1,128)S(1)} %reshape.201.gain_ref, ...), custom_call_target="tpu_custom_call" | custom-call | flops 1000 | bytes 1000 | tf_op jit(solution)/shard_map/attend/pallas_call | solution.py:117
  28.3 17.4 %collective-permute-done.1.other_ref = f32[448,512]{1,0:T(8,128)} collective-permute-done((f32[448,512]{1,0:T(8,128)}, f32[448,512]{1,0:T(8,128)}, u32[]{:S(2)}, u32[]{:S(2)}) %collective-permute-start.1) | collective-permute-done | bytes 917536 | tf_op jit(solution)/shard_map/ppermute | solution.py:43
  45.7 3.3 %project.1 = (f32[512,896]{1,0:T(8,128)S(1)}, bf16[512,896]{1,0:T(8,128)(2,1)S(1)}, f32[256,896]{1,0:T(8,128)S(1)}, f32[256,896]{1,0:T(8,128)S(1)}) custom-call(f32[1,896]{1,0:T(1,128)S(1)} %broadcast_in_dim.30.first_ref, bf16[512,896]{1,0:T(8,128)(2,1)S(1)} %copy-done.2, bf16[512,448]{1,0:T(8,128)(2,1)S(1)} %copy-done.10, ...), custom_call_target="tpu_custom_call" | custom-call | flops 1000 | bytes 1000 | tf_op jit(solution)/shard_map/project/pallas_call | solution.py:117
  53.0 9.1 %ffn_rows.3 = (bf16[512,2432]{1,0:T(8,128)(2,1)S(1)}, bf16[512,2432]{1,0:T(8,128)(2,1)S(1)}, bf16[512,2432]{1,0:T(8,128)(2,1)S(1)}) custom-call(bf16[512,896]{1,0:T(8,128)(2,1)S(1)} %get-tuple-element.107.refs_0_, bf16[512,896]{1,0:T(8,128)(2,1)S(1)} %get-tuple-element.267.refs_1_.refs_0_.refs_6_, bf16[896,2432]{1,0:T(8,128)(2,1)S(1)} %bitcast.17, ...), custom_call_target="tpu_custom_call" | custom-call | flops 1000 | bytes 1000 | tf_op jit(solution)/shard_map/ffn_rows/pallas_call | solution.py:117
  64.1 3.4 %ffn_back.2.refs_0_ = f32[256,896]{1,0:T(8,128)S(1)} custom-call(bf16[512,2432]{1,0:T(8,128)(2,1)S(1)} %get-tuple-element.114.gate_rows_ref.refs_3_, bf16[512,2432]{1,0:T(8,128)(2,1)S(1)} %get-tuple-element.113.up_rows_ref.refs_3_, bf16[896,2432]{1,0:T(8,128)(2,1)S(1)} %bitcast.17, bf16[896,2432]{1,0:T(8,128)(2,1)S(1)} %copy-done), custom_call_target="tpu_custom_call" | custom-call | flops 1000 | bytes 1000 | tf_op jit(solution)/shard_map/ffn_back/pallas_call | solution.py:117
  67.5 3.4 %ffn_back.3.refs_1_ = f32[256,896]{1,0:T(8,128)S(1)} custom-call(bf16[512,2432]{1,0:T(8,128)(2,1)S(1)} %get-tuple-element.114.gate_rows_ref.refs_3_, bf16[512,2432]{1,0:T(8,128)(2,1)S(1)} %get-tuple-element.113.up_rows_ref.refs_3_, bf16[896,2432]{1,0:T(8,128)(2,1)S(1)} %bitcast.17, bf16[896,2432]{1,0:T(8,128)(2,1)S(1)} %copy-done), custom_call_target="tpu_custom_call" | custom-call | flops 1000 | bytes 1000 | tf_op jit(solution)/shard_map/ffn_back/pallas_call | solution.py:117
  75.9 5.0 %ffn_rows.4 = (bf16[256,2432]{1,0:T(8,128)(2,1)S(1)}, bf16[256,2432]{1,0:T(8,128)(2,1)S(1)}, bf16[256,2432]{1,0:T(8,128)(2,1)S(1)}, bf16[256,896]{1,0:T(8,128)(2,1)S(1)}, bf16[256,896]{1,0:T(8,128)(2,1)S(1)}) custom-call(f32[1,896]{1,0:T(1,128)S(1)} %broadcast_in_dim.56.refs_0_, f32[128,896]{1,0:T(8,128)S(1)} %collective-permute-done.3.refs_1_, ...), custom_call_target="tpu_custom_call" | custom-call | flops 1000 | bytes 1000 | tf_op jit(solution)/shard_map/ffn_rows/pallas_call | solution.py:117
  83.4 5.2 %ffn_rows.5 = (bf16[256,2432]{1,0:T(8,128)(2,1)S(1)}, bf16[256,2432]{1,0:T(8,128)(2,1)S(1)}, bf16[256,2432]{1,0:T(8,128)(2,1)S(1)}, bf16[256,896]{1,0:T(8,128)(2,1)S(1)}, bf16[256,896]{1,0:T(8,128)(2,1)S(1)}) custom-call(f32[256,896]{1,0:T(8,128)S(1)} %collective-permute-done.6.refs_0_, f32[256,896]{1,0:T(8,128)S(1)} %get-tuple-element.262.refs_1_, ...), custom_call_target="tpu_custom_call" | custom-call | flops 1000 | bytes 1000 | tf_op jit(solution)/shard_map/ffn_rows/pallas_call | solution.py:117
  92.5 3.3 %ffn_down.1 = (f32[256,896]{1,0:T(8,128)S(1)}, f32[256,896]{1,0:T(8,128)S(1)}) custom-call(bf16[512,2432]{1,0:T(8,128)(2,1)S(1)} %get-tuple-element.126.refs_3_.hidden_ref, bf16[2432,896]{1,0:T(8,128)(2,1)S(1)} %bitcast.19), custom_call_target="tpu_custom_call" | custom-call | flops 1000 | bytes 1000 | tf_op jit(solution)/shard_map/ffn_down/pallas_call | solution.py:117
  102.8 2.8 %outer_fold.3 = (f32[112,2432]{1,0:T(8,128)S(1)}, f32[112,2432]{1,0:T(8,128)S(1)}) custom-call(bf16[224,896]{1,0:T(8,128)(2,1)S(1)} %copy-done.7, bf16[512,896]{1,0:T(8,128)(2,1)S(1)} %get-tuple-element.267.refs_1_.refs_0_.refs_6_, bf16[256,896]{1,0:T(8,128)(2,1)S(1)} %get-tuple-element.116.refs_1_, bf16[256,896]{1,0:T(8,128)(2,1)S(1)} %get-tuple-element.120.refs_2_, ...), custom_call_target="tpu_custom_call" | custom-call | flops 1000 | bytes 1000 | tf_op jit(solution)/shard_map/outer_fold/pallas_call | solution.py:117
  108.3 3.8 %outer_fold.4 = (f32[112,2432]{1,0:T(8,128)S(1)}, f32[112,2432]{1,0:T(8,128)}) custom-call(bf16[224,896]{1,0:T(8,128)(2,1)S(1)} %copy-done.7, bf16[512,896]{1,0:T(8,128)(2,1)S(1)} %get-tuple-element.107.refs_0_, bf16[256,896]{1,0:T(8,128)(2,1)S(1)} %get-tuple-element.130.refs_1_, bf16[256,896]{1,0:T(8,128)(2,1)S(1)} %get-tuple-element.131.refs_2_, ...), custom_call_target="tpu_custom_call" | custom-call | flops 1000 | bytes 1000 | tf_op jit(solution)/shard_map/outer_fold/pallas_call | solution.py:117
  116.5 13.1 %collective-permute-done.17.refs_3_ = f32[256,896]{1,0:T(8,128)S(1)} collective-permute-done((f32[256,896]{1,0:T(8,128)S(1)}, f32[256,896]{1,0:T(8,128)S(1)}, u32[]{:S(2)}, u32[]{:S(2)}) %collective-permute-start.17) | collective-permute-done | bytes 917536 | tf_op jit(solution)/shard_map/ppermute | solution.py:43
  136.0 10.3 %attend_back.1 = (bf16[512,576]{1,0:T(8,128)(2,1)S(1)}, f32[256,896]{1,0:T(8,128)S(1)}, f32[256,896]{1,0:T(8,128)S(1)}, f32[1,896]{1,0:T(1,128)S(1)}) custom-call(bf16[512,896]{1,0:T(8,128)(2,1)S(1)} %get-tuple-element.157.residual_ref, bf16[448,896]{1,0:T(8,128)(2,1)S(1)} %copy-done.8, bf16[576,896]{1,0:T(8,128)(2,1)S(1)} %pad_maximum_fusion.weight_ref, ...), custom_call_target="tpu_custom_call" | custom-call | flops 1000 | bytes 1000 | tf_op jit(solution)/shard_map/attend_back/pallas_call | solution.py:117
  156.0 3.7 %collective-permute-done.25 = f32[56,2432]{1,0:T(8,128)} collective-permute-done((f32[56,2432]{1,0:T(8,128)}, f32[56,2432]{1,0:T(8,128)}, u32[]{:S(2)}, u32[]{:S(2)}) %collective-permute-start.25) | collective-permute-done | bytes 544800 | tf_op jit(solution)/shard_map/ppermute | solution.py:48
  163.1 3.4 %attn_sums.1 = (f32[128,1152]{1,0:T(8,128)S(1)}, f32[128,1152]{1,0:T(8,128)S(1)}, f32[128,1152]{1,0:T(8,128)S(1)}, f32[128,1152]{1,0:T(8,128)S(1)}) custom-call(bf16[512,896]{1,0:T(8,128)(2,1)S(1)} %copy-done.18, f32[896,64]{1,0:T(8,128)S(1)} %pad_bitcast_fusion.gains_ref, bf16[512,896]{1,0:T(8,128)(2,1)S(1)} %copy-done.15, bf16[512,896]{1,0:T(8,128)(2,1)S(1)} %copy-done.4, ...), custom_call_target="tpu_custom_call" | custom-call | flops 1000 | bytes 1000 | tf_op jit(solution)/shard_map/attn_sums/pallas_call | solution.py:117
  168.5 4.9 %collective-permute-done.24.low_x_ref = f32[256,896]{1,0:T(8,128)} collective-permute-done((f32[256,896]{1,0:T(8,128)}, f32[256,896]{1,0:T(8,128)}, u32[]{:S(2)}, u32[]{:S(2)}) %collective-permute-start.24) | collective-permute-done | bytes 917536 | tf_op jit(solution)/shard_map/ppermute | solution.py:43
  176.5 3.4 %attn_fold.1 = (f32[256,1152]{1,0:T(8,128)S(1)}, f32[256,1152]{1,0:T(8,128)S(1)}) custom-call(bf16[512,896]{1,0:T(8,128)(2,1)S(1)} %copy-done.17, f32[896,64]{1,0:T(8,128)S(1)} %pad_bitcast_fusion.gains_ref, bf16[512,896]{1,0:T(8,128)(2,1)S(1)} %copy-done.16, bf16[512,896]{1,0:T(8,128)(2,1)S(1)} %copy-done.4, bf16[512,576]{1,0:T(8,128)(2,1)S(1)} %copy-done.21, ...), custom_call_target="tpu_custom_call" | custom-call | flops 1000 | bytes 1000 | tf_op jit(solution)/shard_map/attn_fold/pallas_call | solution.py:117
  181.6 13.7 %collective-permute-done.35 = f32[56,2432]{1,0:T(8,128)S(1)} collective-permute-done((f32[56,2432]{1,0:T(8,128)S(1)}, f32[56,2432]{1,0:T(8,128)S(1)}, u32[]{:S(2)}, u32[]{:S(2)}) %collective-permute-start.35) | collective-permute-done | bytes 544800 | tf_op jit(solution)/shard_map/ppermute | solution.py:48
  200.5 3.7 %tokens_back.1 = bf16[512,896]{1,0:T(8,128)(2,1)} custom-call(bf16[512,896]{1,0:T(8,128)(2,1)S(1)} %copy-done.2, f32[256,896]{1,0:T(8,128)S(1)} %copy-done.31, f32[256,896]{1,0:T(8,128)S(1)} %copy-done.33, f32[256,896]{1,0:T(8,128)} %collective-permute-done.24.low_x_ref, f32[256,896]{1,0:T(8,128)S(1)} %collective-permute-done.36.high_x_ref, ...), custom_call_target="tpu_custom_call" | custom-call | flops 1000 | bytes 1000 | tf_op jit(solution)/shard_map/tokens_back/pallas_call | solution.py:117
  204.2 3.6 %collective-permute-done.32 = f32[256,1152]{1,0:T(8,128)S(1)} collective-permute-done((f32[256,1152]{1,0:T(8,128)S(1)}, f32[256,1152]{1,0:T(8,128)S(1)}, u32[]{:S(2)}, u32[]{:S(2)}) %collective-permute-start.32) | collective-permute-done | bytes 1179680 | tf_op jit(solution)/shard_map/ppermute | solution.py:48
  208.8 16.6 %collective-permute-done.37 = f32[56,2432]{1,0:T(8,128)S(1)} collective-permute-done((f32[56,2432]{1,0:T(8,128)S(1)}, f32[56,2432]{1,0:T(8,128)S(1)}, u32[]{:S(2)}, u32[]{:S(2)}) %collective-permute-start.37) | collective-permute-done | bytes 544800 | tf_op jit(solution)/shard_map/ppermute | solution.py:48
  227.3 11.6 %collective-permute-done.30 = f32[256,896]{1,0:T(8,128)S(1)} collective-permute-done((f32[256,896]{1,0:T(8,128)S(1)}, f32[256,896]{1,0:T(8,128)S(1)}, u32[]{:S(2)}, u32[]{:S(2)}) %collective-permute-start.30) | collective-permute-done | bytes 917536 | tf_op jit(solution)/shard_map/ppermute | solution.py:43
  241.9 11.7 %collective-permute-done.38 = f32[64,1152]{1,0:T(8,128)S(1)} collective-permute-done((f32[64,1152]{1,0:T(8,128)S(1)}, f32[64,1152]{1,0:T(8,128)S(1)}, u32[]{:S(2)}, u32[]{:S(2)}) %collective-permute-start.38) | collective-permute-done | bytes 294944 | tf_op jit(solution)/shard_map/ppermute | solution.py:48
  (242 shorter events, 89.3 us)
Async XLA Ops:
  2.7 21.2 %collective-permute-start = (f32[224,896]{1,0:T(8,128)}, f32[224,896]{1,0:T(8,128)}, u32[]{:S(2)}, u32[]{:S(2)}) collective-permute-start(f32[224,896]{1,0:T(8,128)} %dynamic-slice_convert_fusion), channel_id=1, source_target_pairs={{0,1},{1,0},{2,3},{3,2},{4,5},{5,4},{6,7},{7,6},{8,9},{9,8},{10,11... | collective-permute-start | bytes 2408456 | tf_op jit(solution)/shard_map/ppermute | solution.py:43
  9.3 54.8 %collective-permute-start.5 = (f32[512,896]{1,0:T(8,128)}, f32[512,896]{1,0:T(8,128)}, u32[]{:S(2)}, u32[]{:S(2)}) collective-permute-start(f32[512,896]{1,0:T(8,128)} %get-tuple-element.266), channel_id=1, source_target_pairs={{0,8},{2,10},{4,12},{6,14},{8,0},{10,2},{12,4},{14,6},{16,24},{18,... | collective-permute-start | bytes 5505032 | tf_op jit(solution)/shard_map/ppermute | solution.py:48
  23.9 21.8 %collective-permute-start.1 = (f32[448,512]{1,0:T(8,128)}, f32[448,512]{1,0:T(8,128)}, u32[]{:S(2)}, u32[]{:S(2)}) collective-permute-start(f32[448,512]{1,0:T(8,128)} %get-tuple-element.103), channel_id=1, source_target_pairs={{0,1},{1,0},{2,3},{3,2},{4,5},{5,4},{6,7},{7,6},{8,9},{9,8},{10,11... | collective-permute-start | bytes 2752520 | tf_op jit(solution)/shard_map/ppermute | solution.py:43
  49.1 12.9 %collective-permute-start.3 = (f32[128,896]{1,0:T(8,128)S(1)}, f32[128,896]{1,0:T(8,128)S(1)}, u32[]{:S(2)}, u32[]{:S(2)}) collective-permute-start(f32[128,896]{1,0:T(8,128)S(1)} %slice_select_fusion), channel_id=1, source_target_pairs={{0,8},{2,10},{4,12},{6,14},{8,0},{10,2},{12,4},{14,6},{16,24},{18,... | collective-permute-start | bytes 1376264 | tf_op jit(solution)/shard_map/ppermute | solution.py:48
  62.1 10.8 %collective-permute-start.4 = (f32[128,896]{1,0:T(8,128)S(1)}, f32[128,896]{1,0:T(8,128)S(1)}, u32[]{:S(2)}, u32[]{:S(2)}) collective-permute-start(f32[128,896]{1,0:T(8,128)S(1)} %collective-permute-done.3.refs_1_), channel_id=1, source_target_pairs={{0,1},{1,0},{2,3},{3,2},{4,5},{5,4},{6,7},{7,6},{8,9},{9,8},{10,11... | collective-permute-start | bytes 1376264 | tf_op jit(solution)/shard_map/ppermute | solution.py:43
  63.6 19.8 %collective-permute-start.6 = (f32[256,896]{1,0:T(8,128)S(1)}, f32[256,896]{1,0:T(8,128)S(1)}, u32[]{:S(2)}, u32[]{:S(2)}) collective-permute-start(f32[256,896]{1,0:T(8,128)S(1)} %get-tuple-element.117), channel_id=1, source_target_pairs={{0,8},{2,10},{4,12},{6,14},{8,0},{10,2},{12,4},{14,6},{16,24},{18,... | collective-permute-start | bytes 2752520 | tf_op jit(solution)/shard_map/ppermute | solution.py:48
  72.8 23.1 %collective-permute-start.7 = (f32[256,896]{1,0:T(8,128)S(1)}, f32[256,896]{1,0:T(8,128)S(1)}, u32[]{:S(2)}, u32[]{:S(2)}) collective-permute-start(f32[256,896]{1,0:T(8,128)S(1)} %ffn_back.2.refs_0_), channel_id=1, source_target_pairs={{0,1},{1,0},{2,3},{3,2},{4,5},{5,4},{6,7},{7,6},{8,9},{9,8},{10,11... | collective-permute-start | bytes 2752520 | tf_op jit(solution)/shard_map/ppermute | solution.py:43
  91.5 10.6 %collective-permute-start.9 = (f32[56,2432]{1,0:T(8,128)S(1)}, f32[56,2432]{1,0:T(8,128)S(1)}, u32[]{:S(2)}, u32[]{:S(2)}) collective-permute-start(f32[56,2432]{1,0:T(8,128)S(1)} %get-tuple-element.123), channel_id=1, source_target_pairs={{0,2},{2,0},{4,6},{6,4},{8,10},{10,8},{12,14},{14,12},{16,18},{18,... | collective-permute-start | bytes 1634312 | tf_op jit(solution)/shard_map/ppermute | solution.py:48
  92.0 10.3 %collective-permute-start.10 = (f32[56,2432]{1,0:T(8,128)S(1)}, f32[56,2432]{1,0:T(8,128)S(1)}, u32[]{:S(2)}, u32[]{:S(2)}) collective-permute-start(f32[56,2432]{1,0:T(8,128)S(1)} %get-tuple-element.124), channel_id=1, source_target_pairs={{0,2},{2,0},{4,6},{6,4},{8,10},{10,8},{12,14},{14,12},{16,18},{18,... | collective-permute-start | bytes 1634312 | tf_op jit(solution)/shard_map/ppermute | solution.py:48
  92.1 10.6 %collective-permute-start.11 = (f32[56,2432]{1,0:T(8,128)S(1)}, f32[56,2432]{1,0:T(8,128)S(1)}, u32[]{:S(2)}, u32[]{:S(2)}) collective-permute-start(f32[56,2432]{1,0:T(8,128)S(1)} %get-tuple-element.125), channel_id=1, source_target_pairs={{0,2},{2,0},{4,6},{6,4},{8,10},{10,8},{12,14},{14,12},{16,18},{18,... | collective-permute-start | bytes 1634312 | tf_op jit(solution)/shard_map/ppermute | solution.py:48
  105.6 27.0 %collective-permute-start.22 = (f32[112,2432]{1,0:T(8,128)S(1)}, f32[112,2432]{1,0:T(8,128)S(1)}, u32[]{:S(2)}, u32[]{:S(2)}) collective-permute-start(f32[112,2432]{1,0:T(8,128)S(1)} %get-tuple-element.146), channel_id=1, source_target_pairs={{0,4},{2,6},{4,0},{6,2},{8,12},{10,14},{12,8},{14,10},{16,20},{18,... | collective-permute-start | bytes 3268616 | tf_op jit(solution)/shard_map/ppermute | solution.py:48
  107.2 22.4 %collective-permute-start.17 = (f32[256,896]{1,0:T(8,128)S(1)}, f32[256,896]{1,0:T(8,128)S(1)}, u32[]{:S(2)}, u32[]{:S(2)}) collective-permute-start(f32[256,896]{1,0:T(8,128)S(1)} %ffn_back.3.refs_1_), channel_id=1, source_target_pairs={{0,1},{1,0},{2,3},{3,2},{4,5},{5,4},{6,7},{7,6},{8,9},{9,8},{10,11... | collective-permute-start | bytes 2752520 | tf_op jit(solution)/shard_map/ppermute | solution.py:43
  113.1 53.5 %collective-permute-start.16 = (f32[112,2432]{1,0:T(8,128)}, f32[112,2432]{1,0:T(8,128)}, u32[]{:S(2)}, u32[]{:S(2)}) collective-permute-start(f32[112,2432]{1,0:T(8,128)} %get-tuple-element.149), channel_id=1, source_target_pairs={{0,4},{2,6},{4,0},{6,2},{8,12},{10,14},{12,8},{14,10},{16,20},{18,... | collective-permute-start | bytes 3268616 | tf_op jit(solution)/shard_map/ppermute | solution.py:48
  133.4 26.2 %collective-permute-start.25 = (f32[56,2432]{1,0:T(8,128)}, f32[56,2432]{1,0:T(8,128)}, u32[]{:S(2)}, u32[]{:S(2)}) collective-permute-start(f32[56,2432]{1,0:T(8,128)} %slice_add_fusion.5), channel_id=1, source_target_pairs={{0,16},{2,18},{4,20},{6,22},{8,24},{10,26},{12,28},{14,30},{16,0},... | collective-permute-start | bytes 1634312 | tf_op jit(solution)/shard_map/ppermute | solution.py:48
  152.8 20.6 %collective-permute-start.24 = (f32[256,896]{1,0:T(8,128)}, f32[256,896]{1,0:T(8,128)}, u32[]{:S(2)}, u32[]{:S(2)}) collective-permute-start(f32[256,896]{1,0:T(8,128)} %copy-done.30), channel_id=1, source_target_pairs={{0,1},{1,0},{2,3},{3,2},{4,5},{5,4},{6,7},{7,6},{8,9},{9,8},{10,11... | collective-permute-start | bytes 2752520 | tf_op jit(solution)/shard_map/ppermute | solution.py:43
  154.0 43.7 %collective-permute-start.33 = (f32[112,2432]{1,0:T(8,128)}, f32[112,2432]{1,0:T(8,128)}, u32[]{:S(2)}, u32[]{:S(2)}) collective-permute-start(f32[112,2432]{1,0:T(8,128)} %copy-done.42), channel_id=1, source_target_pairs={{0,4},{2,6},{4,0},{6,2},{8,12},{10,14},{12,8},{14,10},{16,20},{18,... | collective-permute-start | bytes 3268616 | tf_op jit(solution)/shard_map/ppermute | solution.py:48
  167.9 27.4 %collective-permute-start.35 = (f32[56,2432]{1,0:T(8,128)S(1)}, f32[56,2432]{1,0:T(8,128)S(1)}, u32[]{:S(2)}, u32[]{:S(2)}) collective-permute-start(f32[56,2432]{1,0:T(8,128)S(1)} %slice_add_fusion.3), channel_id=1, source_target_pairs={{0,16},{2,18},{4,20},{6,22},{8,24},{10,26},{12,28},{14,30},{16,0},... | collective-permute-start | bytes 1634312 | tf_op jit(solution)/shard_map/ppermute | solution.py:48
  175.9 24.6 %collective-permute-start.36 = (f32[256,896]{1,0:T(8,128)S(1)}, f32[256,896]{1,0:T(8,128)S(1)}, u32[]{:S(2)}, u32[]{:S(2)}) collective-permute-start(f32[256,896]{1,0:T(8,128)S(1)} %copy-done.33), channel_id=1, source_target_pairs={{0,1},{1,0},{2,3},{3,2},{4,5},{5,4},{6,7},{7,6},{8,9},{9,8},{10,11... | collective-permute-start | bytes 2752520 | tf_op jit(solution)/shard_map/ppermute | solution.py:43
  179.9 27.9 %collective-permute-start.32 = (f32[256,1152]{1,0:T(8,128)S(1)}, f32[256,1152]{1,0:T(8,128)S(1)}, u32[]{:S(2)}, u32[]{:S(2)}) collective-permute-start(f32[256,1152]{1,0:T(8,128)S(1)} %get-tuple-element.173), channel_id=1, source_target_pairs={{0,4},{2,6},{4,0},{6,2},{8,12},{10,14},{12,8},{14,10},{16,20},{18,... | collective-permute-start | bytes 3538952 | tf_op jit(solution)/shard_map/ppermute | solution.py:48
  197.2 41.9 %collective-permute-start.31 = (f32[256,896]{1,0:T(8,128)S(1)}, f32[256,896]{1,0:T(8,128)S(1)}, u32[]{:S(2)}, u32[]{:S(2)}) collective-permute-start(f32[256,896]{1,0:T(8,128)S(1)} %copy-done.35), channel_id=1, source_target_pairs={{0,1},{1,0},{2,3},{3,2},{4,5},{5,4},{6,7},{7,6},{8,9},{9,8},{10,11... | collective-permute-start | bytes 2752520 | tf_op jit(solution)/shard_map/ppermute | solution.py:43
  197.7 41.2 %collective-permute-start.30 = (f32[256,896]{1,0:T(8,128)S(1)}, f32[256,896]{1,0:T(8,128)S(1)}, u32[]{:S(2)}, u32[]{:S(2)}) collective-permute-start(f32[256,896]{1,0:T(8,128)S(1)} %copy-done.37), channel_id=1, source_target_pairs={{0,1},{1,0},{2,3},{3,2},{4,5},{5,4},{6,7},{7,6},{8,9},{9,8},{10,11... | collective-permute-start | bytes 2752520 | tf_op jit(solution)/shard_map/ppermute | solution.py:43
  200.4 25.1 %collective-permute-start.37 = (f32[56,2432]{1,0:T(8,128)S(1)}, f32[56,2432]{1,0:T(8,128)S(1)}, u32[]{:S(2)}, u32[]{:S(2)}) collective-permute-start(f32[56,2432]{1,0:T(8,128)S(1)} %slice_add_fusion.4), channel_id=1, source_target_pairs={{0,16},{2,18},{4,20},{6,22},{8,24},{10,26},{12,28},{14,30},{16,0},... | collective-permute-start | bytes 1634312 | tf_op jit(solution)/shard_map/ppermute | solution.py:48
  207.9 31.1 %collective-permute-start.34 = (f32[128,1152]{1,0:T(8,128)S(1)}, f32[128,1152]{1,0:T(8,128)S(1)}, u32[]{:S(2)}, u32[]{:S(2)}) collective-permute-start(f32[128,1152]{1,0:T(8,128)S(1)} %get-tuple-element.260), channel_id=1, source_target_pairs={{0,8},{2,10},{4,12},{6,14},{8,0},{10,2},{12,4},{14,6},{16,24},{18,... | collective-permute-start | bytes 1769480 | tf_op jit(solution)/shard_map/ppermute | solution.py:48
  239.3 14.4 %collective-permute-start.38 = (f32[64,1152]{1,0:T(8,128)S(1)}, f32[64,1152]{1,0:T(8,128)S(1)}, u32[]{:S(2)}, u32[]{:S(2)}) collective-permute-start(f32[64,1152]{1,0:T(8,128)S(1)} %slice_add_fusion.7), channel_id=1, source_target_pairs={{0,16},{2,18},{4,20},{6,22},{8,24},{10,26},{12,28},{14,30},{16,0},... | collective-permute-start | bytes 884744 | tf_op jit(solution)/shard_map/ppermute | solution.py:48
  (72 other events, 673.4 us)

commit v2 on v1

--- a/solution.py
+++ b/solution.py
@@ -90,7 +90,7 @@
 IN_VMEM = pl.BlockSpec(memory_space=pltpu.VMEM)
 LIMIT = 11
 EXTRA = 8
-ROWS = 64
+ROWS = 128
 CUTS = 4
 ATTN_CUTS = 4
 

time: 258 us -> 272 us (1.054); the launches traced: 258 us -> 267 us
  Pallas kernels: 80.2 us -> 87.7 us
    pallas_call x19, Pallas kernels: 80.2 us -> 87.7 us  [call(): pl.pallas_call(kernel, in_specs=[IN_VMEM] * len(operands), out_specs=[IN_...]
  transfers between devices with their start and end apart: 39 -> 39, of which waited for: 14 -> 14; matrix products, arithmetic and copies ran while one was open for 9% -> 8% of each run, Pallas kernels for 31% -> 33%
where the time goes in v2:
time: 272 us; the launch traced here: 267 us
  waiting for transfers between devices  106 us (39%)
  Pallas kernels  87.7 us (32%)
  starting transfers between devices  28.8 us (11%)
  local copies, waits for them, and re-layouts  22.8 us (8%)
  other arithmetic  19.7 us (7%)
    pallas_call x19, Pallas kernels, call(): pl.pallas_call(kernel, in_specs=[IN_VMEM] * len(operands), out_specs=[IN_...  87.7 us
    ppermute x10, waiting for transfers between devices, swap_tensor(): return lax.ppermute(rows, 'tensor', [(i, i ^ 1) for i in range(size)])  53 us
    ppermute x29, waiting for transfers between devices, swap_dp(): return lax.ppermute(rows, 'dp', [(i, i ^ 1 << bit) for i in range(size)])  52.6 us
    ppermute x29, starting transfers between devices, swap_dp(): return lax.ppermute(rows, 'dp', [(i, i ^ 1 << bit) for i in range(size)])  16.7 us
    unnamed x115, local copies, waits for them, and re-layouts  14.6 us
    ppermute x10, starting transfers between devices, swap_tensor(): return lax.ppermute(rows, 'tensor', [(i, i ^ 1) for i in range(size)])  12.1 us
  transfers between devices with their start and end apart: 39, of which 14 were waited for; matrix products, arithmetic and copies ran while one was open for 8% of the time, Pallas kernels for 33%

profile of v2, /device:TPU:0, one launch (start us, length us, event | category | flops | bytes accessed | tf_op | source)
XLA Modules:
  0.0 266.5 jit_solution(2045349535174991430)
XLA Ops:
  2.7 3.0 %collective-permute-start = (f32[224,896]{1,0:T(8,128)}, f32[224,896]{1,0:T(8,128)}, u32[]{:S(2)}, u32[]{:S(2)}) collective-permute-start(f32[224,896]{1,0:T(8,128)} %dynamic-slice_convert_fusion), channel_id=1, source_target_pairs={{0,1},{1,0},{2,3},{3,2},{4,5},{5,4},{6,7},{7,6},{8,9},{9,8},{10,11... | collective-permute-start | bytes 2408456 | tf_op jit(solution)/shard_map/ppermute | solution.py:43
  13.0 7.3 %attend.1 = (bf16[512,896]{1,0:T(8,128)(2,1)S(1)}, bf16[576,512]{1,0:T(8,128)(2,1)S(1)}, bf16[512,448]{1,0:T(8,128)(2,1)S(1)}, f32[448,512]{1,0:T(8,128)}, f32[8,512]{1,0:T(8,128)S(1)}, /*index=5*/f32[8,512]{1,0:T(8,128)S(1)}) custom-call(bf16[512,896]{1,0:T(8,128)(2,1)S(1)} %copy-done.2, f32[1,896]{1,0:T(1,128)S(1)} %reshape.201.gain_ref, ...), custom_call_target="tpu_custom_call" | custom-call | flops 1000 | bytes 1000 | tf_op jit(solution)/shard_map/attend/pallas_call | solution.py:117
  28.3 17.4 %collective-permute-done.1.other_ref = f32[448,512]{1,0:T(8,128)} collective-permute-done((f32[448,512]{1,0:T(8,128)}, f32[448,512]{1,0:T(8,128)}, u32[]{:S(2)}, u32[]{:S(2)}) %collective-permute-start.1) | collective-permute-done | bytes 917536 | tf_op jit(solution)/shard_map/ppermute | solution.py:43
  45.7 3.3 %project.1 = (f32[512,896]{1,0:T(8,128)S(1)}, bf16[512,896]{1,0:T(8,128)(2,1)S(1)}, f32[256,896]{1,0:T(8,128)S(1)}, f32[256,896]{1,0:T(8,128)S(1)}) custom-call(f32[1,896]{1,0:T(1,128)S(1)} %broadcast_in_dim.30.first_ref, bf16[512,896]{1,0:T(8,128)(2,1)S(1)} %copy-done.2, bf16[512,448]{1,0:T(8,128)(2,1)S(1)} %copy-done.10, ...), custom_call_target="tpu_custom_call" | custom-call | flops 1000 | bytes 1000 | tf_op jit(solution)/shard_map/project/pallas_call | solution.py:117
  53.0 9.1 %ffn_rows.3 = (bf16[512,2432]{1,0:T(8,128)(2,1)S(1)}, bf16[512,2432]{1,0:T(8,128)(2,1)S(1)}, bf16[512,2432]{1,0:T(8,128)(2,1)S(1)}) custom-call(bf16[512,896]{1,0:T(8,128)(2,1)S(1)} %get-tuple-element.107.refs_0_, bf16[512,896]{1,0:T(8,128)(2,1)S(1)} %get-tuple-element.267.refs_1_.refs_0_.refs_6_, bf16[896,2432]{1,0:T(8,128)(2,1)S(1)} %bitcast.17, ...), custom_call_target="tpu_custom_call" | custom-call | flops 1000 | bytes 1000 | tf_op jit(solution)/shard_map/ffn_rows/pallas_call | solution.py:117
  64.1 3.4 %ffn_back.2.refs_0_ = f32[256,896]{1,0:T(8,128)S(1)} custom-call(bf16[512,2432]{1,0:T(8,128)(2,1)S(1)} %get-tuple-element.114.gate_rows_ref.refs_3_, bf16[512,2432]{1,0:T(8,128)(2,1)S(1)} %get-tuple-element.113.up_rows_ref.refs_3_, bf16[896,2432]{1,0:T(8,128)(2,1)S(1)} %bitcast.17, bf16[896,2432]{1,0:T(8,128)(2,1)S(1)} %copy-done), custom_call_target="tpu_custom_call" | custom-call | flops 1000 | bytes 1000 | tf_op jit(solution)/shard_map/ffn_back/pallas_call | solution.py:117
  67.5 3.4 %ffn_back.3.refs_1_ = f32[256,896]{1,0:T(8,128)S(1)} custom-call(bf16[512,2432]{1,0:T(8,128)(2,1)S(1)} %get-tuple-element.114.gate_rows_ref.refs_3_, bf16[512,2432]{1,0:T(8,128)(2,1)S(1)} %get-tuple-element.113.up_rows_ref.refs_3_, bf16[896,2432]{1,0:T(8,128)(2,1)S(1)} %bitcast.17, bf16[896,2432]{1,0:T(8,128)(2,1)S(1)} %copy-done), custom_call_target="tpu_custom_call" | custom-call | flops 1000 | bytes 1000 | tf_op jit(solution)/shard_map/ffn_back/pallas_call | solution.py:117
  75.9 5.0 %ffn_rows.4 = (bf16[256,2432]{1,0:T(8,128)(2,1)S(1)}, bf16[256,2432]{1,0:T(8,128)(2,1)S(1)}, bf16[256,2432]{1,0:T(8,128)(2,1)S(1)}, bf16[256,896]{1,0:T(8,128)(2,1)S(1)}, bf16[256,896]{1,0:T(8,128)(2,1)S(1)}) custom-call(f32[1,896]{1,0:T(1,128)S(1)} %broadcast_in_dim.56.refs_0_, f32[128,896]{1,0:T(8,128)S(1)} %collective-permute-done.3.refs_1_, ...), custom_call_target="tpu_custom_call" | custom-call | flops 1000 | bytes 1000 | tf_op jit(solution)/shard_map/ffn_rows/pallas_call | solution.py:117
  83.4 13.6 %ffn_rows.5 = (bf16[256,2432]{1,0:T(8,128)(2,1)S(1)}, bf16[256,2432]{1,0:T(8,128)(2,1)S(1)}, bf16[256,2432]{1,0:T(8,128)(2,1)S(1)}, bf16[256,896]{1,0:T(8,128)(2,1)S(1)}, bf16[256,896]{1,0:T(8,128)(2,1)S(1)}) custom-call(f32[256,896]{1,0:T(8,128)S(1)} %collective-permute-done.6.refs_0_, f32[256,896]{1,0:T(8,128)S(1)} %get-tuple-element.262.refs_1_, ...), custom_call_target="tpu_custom_call" | custom-call | flops 1000 | bytes 1000 | tf_op jit(solution)/shard_map/ffn_rows/pallas_call | solution.py:117
  100.9 3.3 %ffn_down.1 = (f32[256,896]{1,0:T(8,128)S(1)}, f32[256,896]{1,0:T(8,128)S(1)}) custom-call(bf16[512,2432]{1,0:T(8,128)(2,1)S(1)} %get-tuple-element.126.refs_3_.hidden_ref, bf16[2432,896]{1,0:T(8,128)(2,1)S(1)} %bitcast.19), custom_call_target="tpu_custom_call" | custom-call | flops 1000 | bytes 1000 | tf_op jit(solution)/shard_map/ffn_down/pallas_call | solution.py:117
  111.2 2.8 %outer_fold.3 = (f32[112,2432]{1,0:T(8,128)S(1)}, f32[112,2432]{1,0:T(8,128)S(1)}) custom-call(bf16[224,896]{1,0:T(8,128)(2,1)S(1)} %copy-done.7, bf16[512,896]{1,0:T(8,128)(2,1)S(1)} %get-tuple-element.267.refs_1_.refs_0_.refs_6_, bf16[256,896]{1,0:T(8,128)(2,1)S(1)} %get-tuple-element.116.refs_1_, bf16[256,896]{1,0:T(8,128)(2,1)S(1)} %get-tuple-element.120.refs_2_, ...), custom_call_target="tpu_custom_call" | custom-call | flops 1000 | bytes 1000 | tf_op jit(solution)/shard_map/outer_fold/pallas_call | solution.py:117
  116.8 3.8 %outer_fold.4 = (f32[112,2432]{1,0:T(8,128)S(1)}, f32[112,2432]{1,0:T(8,128)}) custom-call(bf16[224,896]{1,0:T(8,128)(2,1)S(1)} %copy-done.7, bf16[512,896]{1,0:T(8,128)(2,1)S(1)} %get-tuple-element.107.refs_0_, bf16[256,896]{1,0:T(8,128)(2,1)S(1)} %get-tuple-element.130.refs_1_, bf16[256,896]{1,0:T(8,128)(2,1)S(1)} %get-tuple-element.131.refs_2_, ...), custom_call_target="tpu_custom_call" | custom-call | flops 1000 | bytes 1000 | tf_op jit(solution)/shard_map/outer_fold/pallas_call | solution.py:117
  124.9 13.1 %collective-permute-done.17.refs_3_ = f32[256,896]{1,0:T(8,128)S(1)} collective-permute-done((f32[256,896]{1,0:T(8,128)S(1)}, f32[256,896]{1,0:T(8,128)S(1)}, u32[]{:S(2)}, u32[]{:S(2)}) %collective-permute-start.17) | collective-permute-done | bytes 917536 | tf_op jit(solution)/shard_map/ppermute | solution.py:43
  144.6 10.3 %attend_back.1 = (bf16[512,576]{1,0:T(8,128)(2,1)S(1)}, f32[256,896]{1,0:T(8,128)S(1)}, f32[256,896]{1,0:T(8,128)S(1)}, f32[1,896]{1,0:T(1,128)S(1)}) custom-call(bf16[512,896]{1,0:T(8,128)(2,1)S(1)} %get-tuple-element.157.residual_ref, bf16[448,896]{1,0:T(8,128)(2,1)S(1)} %copy-done.8, bf16[576,896]{1,0:T(8,128)(2,1)S(1)} %pad_maximum_fusion.weight_ref, ...), custom_call_target="tpu_custom_call" | custom-call | flops 1000 | bytes 1000 | tf_op jit(solution)/shard_map/attend_back/pallas_call | solution.py:117
  164.4 3.6 %collective-permute-done.25 = f32[56,2432]{1,0:T(8,128)} collective-permute-done((f32[56,2432]{1,0:T(8,128)}, f32[56,2432]{1,0:T(8,128)}, u32[]{:S(2)}, u32[]{:S(2)}) %collective-permute-start.25) | collective-permute-done | bytes 544800 | tf_op jit(solution)/shard_map/ppermute | solution.py:48
  171.5 3.4 %attn_sums.1 = (f32[128,1152]{1,0:T(8,128)S(1)}, f32[128,1152]{1,0:T(8,128)S(1)}, f32[128,1152]{1,0:T(8,128)S(1)}, f32[128,1152]{1,0:T(8,128)S(1)}) custom-call(bf16[512,896]{1,0:T(8,128)(2,1)S(1)} %copy-done.18, f32[896,64]{1,0:T(8,128)S(1)} %pad_bitcast_fusion.gains_ref, bf16[512,896]{1,0:T(8,128)(2,1)S(1)} %copy-done.15, bf16[512,896]{1,0:T(8,128)(2,1)S(1)} %copy-done.4, ...), custom_call_target="tpu_custom_call" | custom-call | flops 1000 | bytes 1000 | tf_op jit(solution)/shard_map/attn_sums/pallas_call | solution.py:117
  176.9 4.9 %collective-permute-done.24.low_x_ref = f32[256,896]{1,0:T(8,128)} collective-permute-done((f32[256,896]{1,0:T(8,128)}, f32[256,896]{1,0:T(8,128)}, u32[]{:S(2)}, u32[]{:S(2)}) %collective-permute-start.24) | collective-permute-done | bytes 917536 | tf_op jit(solution)/shard_map/ppermute | solution.py:43
  184.9 3.4 %attn_fold.1 = (f32[256,1152]{1,0:T(8,128)S(1)}, f32[256,1152]{1,0:T(8,128)S(1)}) custom-call(bf16[512,896]{1,0:T(8,128)(2,1)S(1)} %copy-done.17, f32[896,64]{1,0:T(8,128)S(1)} %pad_bitcast_fusion.gains_ref, bf16[512,896]{1,0:T(8,128)(2,1)S(1)} %copy-done.16, bf16[512,896]{1,0:T(8,128)(2,1)S(1)} %copy-done.4, bf16[512,576]{1,0:T(8,128)(2,1)S(1)} %copy-done.21, ...), custom_call_target="tpu_custom_call" | custom-call | flops 1000 | bytes 1000 | tf_op jit(solution)/shard_map/attn_fold/pallas_call | solution.py:117
  190.0 13.7 %collective-permute-done.35 = f32[56,2432]{1,0:T(8,128)S(1)} collective-permute-done((f32[56,2432]{1,0:T(8,128)S(1)}, f32[56,2432]{1,0:T(8,128)S(1)}, u32[]{:S(2)}, u32[]{:S(2)}) %collective-permute-start.35) | collective-permute-done | bytes 544800 | tf_op jit(solution)/shard_map/ppermute | solution.py:48
  208.9 3.4 %tokens_back.1 = bf16[512,896]{1,0:T(8,128)(2,1)} custom-call(bf16[512,896]{1,0:T(8,128)(2,1)S(1)} %copy-done.2, f32[256,896]{1,0:T(8,128)S(1)} %copy-done.31, f32[256,896]{1,0:T(8,128)S(1)} %copy-done.33, f32[256,896]{1,0:T(8,128)} %collective-permute-done.24.low_x_ref, f32[256,896]{1,0:T(8,128)S(1)} %collective-permute-done.36.high_x_ref, ...), custom_call_target="tpu_custom_call" | custom-call | flops 1000 | bytes 1000 | tf_op jit(solution)/shard_map/tokens_back/pallas_call | solution.py:117
  212.3 3.9 %collective-permute-done.32 = f32[256,1152]{1,0:T(8,128)S(1)} collective-permute-done((f32[256,1152]{1,0:T(8,128)S(1)}, f32[256,1152]{1,0:T(8,128)S(1)}, u32[]{:S(2)}, u32[]{:S(2)}) %collective-permute-start.32) | collective-permute-done | bytes 1179680 | tf_op jit(solution)/shard_map/ppermute | solution.py:48
  217.2 16.6 %collective-permute-done.37 = f32[56,2432]{1,0:T(8,128)S(1)} collective-permute-done((f32[56,2432]{1,0:T(8,128)S(1)}, f32[56,2432]{1,0:T(8,128)S(1)}, u32[]{:S(2)}, u32[]{:S(2)}) %collective-permute-start.37) | collective-permute-done | bytes 544800 | tf_op jit(solution)/shard_map/ppermute | solution.py:48
  235.7 11.6 %collective-permute-done.30 = f32[256,896]{1,0:T(8,128)S(1)} collective-permute-done((f32[256,896]{1,0:T(8,128)S(1)}, f32[256,896]{1,0:T(8,128)S(1)}, u32[]{:S(2)}, u32[]{:S(2)}) %collective-permute-start.30) | collective-permute-done | bytes 917536 | tf_op jit(solution)/shard_map/ppermute | solution.py:43
  250.3 11.7 %collective-permute-done.38 = f32[64,1152]{1,0:T(8,128)S(1)} collective-permute-done((f32[64,1152]{1,0:T(8,128)S(1)}, f32[64,1152]{1,0:T(8,128)S(1)}, u32[]{:S(2)}, u32[]{:S(2)}) %collective-permute-start.38) | collective-permute-done | bytes 294944 | tf_op jit(solution)/shard_map/ppermute | solution.py:48
  (242 shorter events, 89.7 us)
Async XLA Ops:
  2.7 21.2 %collective-permute-start = (f32[224,896]{1,0:T(8,128)}, f32[224,896]{1,0:T(8,128)}, u32[]{:S(2)}, u32[]{:S(2)}) collective-permute-start(f32[224,896]{1,0:T(8,128)} %dynamic-slice_convert_fusion), channel_id=1, source_target_pairs={{0,1},{1,0},{2,3},{3,2},{4,5},{5,4},{6,7},{7,6},{8,9},{9,8},{10,11... | collective-permute-start | bytes 2408456 | tf_op jit(solution)/shard_map/ppermute | solution.py:43
  9.3 54.8 %collective-permute-start.5 = (f32[512,896]{1,0:T(8,128)}, f32[512,896]{1,0:T(8,128)}, u32[]{:S(2)}, u32[]{:S(2)}) collective-permute-start(f32[512,896]{1,0:T(8,128)} %get-tuple-element.266), channel_id=1, source_target_pairs={{0,8},{2,10},{4,12},{6,14},{8,0},{10,2},{12,4},{14,6},{16,24},{18,... | collective-permute-start | bytes 5505032 | tf_op jit(solution)/shard_map/ppermute | solution.py:48
  23.9 21.8 %collective-permute-start.1 = (f32[448,512]{1,0:T(8,128)}, f32[448,512]{1,0:T(8,128)}, u32[]{:S(2)}, u32[]{:S(2)}) collective-permute-start(f32[448,512]{1,0:T(8,128)} %get-tuple-element.103), channel_id=1, source_target_pairs={{0,1},{1,0},{2,3},{3,2},{4,5},{5,4},{6,7},{7,6},{8,9},{9,8},{10,11... | collective-permute-start | bytes 2752520 | tf_op jit(solution)/shard_map/ppermute | solution.py:43
  49.1 12.9 %collective-permute-start.3 = (f32[128,896]{1,0:T(8,128)S(1)}, f32[128,896]{1,0:T(8,128)S(1)}, u32[]{:S(2)}, u32[]{:S(2)}) collective-permute-start(f32[128,896]{1,0:T(8,128)S(1)} %slice_select_fusion), channel_id=1, source_target_pairs={{0,8},{2,10},{4,12},{6,14},{8,0},{10,2},{12,4},{14,6},{16,24},{18,... | collective-permute-start | bytes 1376264 | tf_op jit(solution)/shard_map/ppermute | solution.py:48
  62.1 10.8 %collective-permute-start.4 = (f32[128,896]{1,0:T(8,128)S(1)}, f32[128,896]{1,0:T(8,128)S(1)}, u32[]{:S(2)}, u32[]{:S(2)}) collective-permute-start(f32[128,896]{1,0:T(8,128)S(1)} %collective-permute-done.3.refs_1_), channel_id=1, source_target_pairs={{0,1},{1,0},{2,3},{3,2},{4,5},{5,4},{6,7},{7,6},{8,9},{9,8},{10,11... | collective-permute-start | bytes 1376264 | tf_op jit(solution)/shard_map/ppermute | solution.py:43
  63.6 19.8 %collective-permute-start.6 = (f32[256,896]{1,0:T(8,128)S(1)}, f32[256,896]{1,0:T(8,128)S(1)}, u32[]{:S(2)}, u32[]{:S(2)}) collective-permute-start(f32[256,896]{1,0:T(8,128)S(1)} %get-tuple-element.117), channel_id=1, source_target_pairs={{0,8},{2,10},{4,12},{6,14},{8,0},{10,2},{12,4},{14,6},{16,24},{18,... | collective-permute-start | bytes 2752520 | tf_op jit(solution)/shard_map/ppermute | solution.py:48
  72.8 31.5 %collective-permute-start.7 = (f32[256,896]{1,0:T(8,128)S(1)}, f32[256,896]{1,0:T(8,128)S(1)}, u32[]{:S(2)}, u32[]{:S(2)}) collective-permute-start(f32[256,896]{1,0:T(8,128)S(1)} %ffn_back.2.refs_0_), channel_id=1, source_target_pairs={{0,1},{1,0},{2,3},{3,2},{4,5},{5,4},{6,7},{7,6},{8,9},{9,8},{10,11... | collective-permute-start | bytes 2752520 | tf_op jit(solution)/shard_map/ppermute | solution.py:43
  99.9 10.6 %collective-permute-start.9 = (f32[56,2432]{1,0:T(8,128)S(1)}, f32[56,2432]{1,0:T(8,128)S(1)}, u32[]{:S(2)}, u32[]{:S(2)}) collective-permute-start(f32[56,2432]{1,0:T(8,128)S(1)} %get-tuple-element.123), channel_id=1, source_target_pairs={{0,2},{2,0},{4,6},{6,4},{8,10},{10,8},{12,14},{14,12},{16,18},{18,... | collective-permute-start | bytes 1634312 | tf_op jit(solution)/shard_map/ppermute | solution.py:48
  100.4 10.3 %collective-permute-start.10 = (f32[56,2432]{1,0:T(8,128)S(1)}, f32[56,2432]{1,0:T(8,128)S(1)}, u32[]{:S(2)}, u32[]{:S(2)}) collective-permute-start(f32[56,2432]{1,0:T(8,128)S(1)} %get-tuple-element.124), channel_id=1, source_target_pairs={{0,2},{2,0},{4,6},{6,4},{8,10},{10,8},{12,14},{14,12},{16,18},{18,... | collective-permute-start | bytes 1634312 | tf_op jit(solution)/shard_map/ppermute | solution.py:48
  100.5 10.6 %collective-permute-start.11 = (f32[56,2432]{1,0:T(8,128)S(1)}, f32[56,2432]{1,0:T(8,128)S(1)}, u32[]{:S(2)}, u32[]{:S(2)}) collective-permute-start(f32[56,2432]{1,0:T(8,128)S(1)} %get-tuple-element.125), channel_id=1, source_target_pairs={{0,2},{2,0},{4,6},{6,4},{8,10},{10,8},{12,14},{14,12},{16,18},{18,... | collective-permute-start | bytes 1634312 | tf_op jit(solution)/shard_map/ppermute | solution.py:48
  114.0 27.0 %collective-permute-start.22 = (f32[112,2432]{1,0:T(8,128)S(1)}, f32[112,2432]{1,0:T(8,128)S(1)}, u32[]{:S(2)}, u32[]{:S(2)}) collective-permute-start(f32[112,2432]{1,0:T(8,128)S(1)} %get-tuple-element.146), channel_id=1, source_target_pairs={{0,4},{2,6},{4,0},{6,2},{8,12},{10,14},{12,8},{14,10},{16,20},{18,... | collective-permute-start | bytes 3268616 | tf_op jit(solution)/shard_map/ppermute | solution.py:48
  115.6 22.4 %collective-permute-start.17 = (f32[256,896]{1,0:T(8,128)S(1)}, f32[256,896]{1,0:T(8,128)S(1)}, u32[]{:S(2)}, u32[]{:S(2)}) collective-permute-start(f32[256,896]{1,0:T(8,128)S(1)} %ffn_back.3.refs_1_), channel_id=1, source_target_pairs={{0,1},{1,0},{2,3},{3,2},{4,5},{5,4},{6,7},{7,6},{8,9},{9,8},{10,11... | collective-permute-start | bytes 2752520 | tf_op jit(solution)/shard_map/ppermute | solution.py:43
  121.6 53.4 %collective-permute-start.16 = (f32[112,2432]{1,0:T(8,128)}, f32[112,2432]{1,0:T(8,128)}, u32[]{:S(2)}, u32[]{:S(2)}) collective-permute-start(f32[112,2432]{1,0:T(8,128)} %get-tuple-element.149), channel_id=1, source_target_pairs={{0,4},{2,6},{4,0},{6,2},{8,12},{10,14},{12,8},{14,10},{16,20},{18,... | collective-permute-start | bytes 3268616 | tf_op jit(solution)/shard_map/ppermute | solution.py:48
  142.0 26.0 %collective-permute-start.25 = (f32[56,2432]{1,0:T(8,128)}, f32[56,2432]{1,0:T(8,128)}, u32[]{:S(2)}, u32[]{:S(2)}) collective-permute-start(f32[56,2432]{1,0:T(8,128)} %slice_add_fusion.5), channel_id=1, source_target_pairs={{0,16},{2,18},{4,20},{6,22},{8,24},{10,26},{12,28},{14,30},{16,0},... | collective-permute-start | bytes 1634312 | tf_op jit(solution)/shard_map/ppermute | solution.py:48
  161.3 20.5 %collective-permute-start.24 = (f32[256,896]{1,0:T(8,128)}, f32[256,896]{1,0:T(8,128)}, u32[]{:S(2)}, u32[]{:S(2)}) collective-permute-start(f32[256,896]{1,0:T(8,128)} %copy-done.30), channel_id=1, source_target_pairs={{0,1},{1,0},{2,3},{3,2},{4,5},{5,4},{6,7},{7,6},{8,9},{9,8},{10,11... | collective-permute-start | bytes 2752520 | tf_op jit(solution)/shard_map/ppermute | solution.py:43
  162.6 43.6 %collective-permute-start.33 = (f32[112,2432]{1,0:T(8,128)}, f32[112,2432]{1,0:T(8,128)}, u32[]{:S(2)}, u32[]{:S(2)}) collective-permute-start(f32[112,2432]{1,0:T(8,128)} %copy-done.42), channel_id=1, source_target_pairs={{0,4},{2,6},{4,0},{6,2},{8,12},{10,14},{12,8},{14,10},{16,20},{18,... | collective-permute-start | bytes 3268616 | tf_op jit(solution)/shard_map/ppermute | solution.py:48
  176.3 27.4 %collective-permute-start.35 = (f32[56,2432]{1,0:T(8,128)S(1)}, f32[56,2432]{1,0:T(8,128)S(1)}, u32[]{:S(2)}, u32[]{:S(2)}) collective-permute-start(f32[56,2432]{1,0:T(8,128)S(1)} %slice_add_fusion.3), channel_id=1, source_target_pairs={{0,16},{2,18},{4,20},{6,22},{8,24},{10,26},{12,28},{14,30},{16,0},... | collective-permute-start | bytes 1634312 | tf_op jit(solution)/shard_map/ppermute | solution.py:48
  184.2 24.6 %collective-permute-start.36 = (f32[256,896]{1,0:T(8,128)S(1)}, f32[256,896]{1,0:T(8,128)S(1)}, u32[]{:S(2)}, u32[]{:S(2)}) collective-permute-start(f32[256,896]{1,0:T(8,128)S(1)} %copy-done.33), channel_id=1, source_target_pairs={{0,1},{1,0},{2,3},{3,2},{4,5},{5,4},{6,7},{7,6},{8,9},{9,8},{10,11... | collective-permute-start | bytes 2752520 | tf_op jit(solution)/shard_map/ppermute | solution.py:43
  188.3 27.9 %collective-permute-start.32 = (f32[256,1152]{1,0:T(8,128)S(1)}, f32[256,1152]{1,0:T(8,128)S(1)}, u32[]{:S(2)}, u32[]{:S(2)}) collective-permute-start(f32[256,1152]{1,0:T(8,128)S(1)} %get-tuple-element.173), channel_id=1, source_target_pairs={{0,4},{2,6},{4,0},{6,2},{8,12},{10,14},{12,8},{14,10},{16,20},{18,... | collective-permute-start | bytes 3538952 | tf_op jit(solution)/shard_map/ppermute | solution.py:48
  205.6 41.9 %collective-permute-start.31 = (f32[256,896]{1,0:T(8,128)S(1)}, f32[256,896]{1,0:T(8,128)S(1)}, u32[]{:S(2)}, u32[]{:S(2)}) collective-permute-start(f32[256,896]{1,0:T(8,128)S(1)} %copy-done.35), channel_id=1, source_target_pairs={{0,1},{1,0},{2,3},{3,2},{4,5},{5,4},{6,7},{7,6},{8,9},{9,8},{10,11... | collective-permute-start | bytes 2752520 | tf_op jit(solution)/shard_map/ppermute | solution.py:43
  206.1 41.2 %collective-permute-start.30 = (f32[256,896]{1,0:T(8,128)S(1)}, f32[256,896]{1,0:T(8,128)S(1)}, u32[]{:S(2)}, u32[]{:S(2)}) collective-permute-start(f32[256,896]{1,0:T(8,128)S(1)} %copy-done.37), channel_id=1, source_target_pairs={{0,1},{1,0},{2,3},{3,2},{4,5},{5,4},{6,7},{7,6},{8,9},{9,8},{10,11... | collective-permute-start | bytes 2752520 | tf_op jit(solution)/shard_map/ppermute | solution.py:43
  208.7 25.1 %collective-permute-start.37 = (f32[56,2432]{1,0:T(8,128)S(1)}, f32[56,2432]{1,0:T(8,128)S(1)}, u32[]{:S(2)}, u32[]{:S(2)}) collective-permute-start(f32[56,2432]{1,0:T(8,128)S(1)} %slice_add_fusion.4), channel_id=1, source_target_pairs={{0,16},{2,18},{4,20},{6,22},{8,24},{10,26},{12,28},{14,30},{16,0},... | collective-permute-start | bytes 1634312 | tf_op jit(solution)/shard_map/ppermute | solution.py:48
  216.3 31.1 %collective-permute-start.34 = (f32[128,1152]{1,0:T(8,128)S(1)}, f32[128,1152]{1,0:T(8,128)S(1)}, u32[]{:S(2)}, u32[]{:S(2)}) collective-permute-start(f32[128,1152]{1,0:T(8,128)S(1)} %get-tuple-element.260), channel_id=1, source_target_pairs={{0,8},{2,10},{4,12},{6,14},{8,0},{10,2},{12,4},{14,6},{16,24},{18,... | collective-permute-start | bytes 1769480 | tf_op jit(solution)/shard_map/ppermute | solution.py:48
  247.6 14.4 %collective-permute-start.38 = (f32[64,1152]{1,0:T(8,128)S(1)}, f32[64,1152]{1,0:T(8,128)S(1)}, u32[]{:S(2)}, u32[]{:S(2)}) collective-permute-start(f32[64,1152]{1,0:T(8,128)S(1)} %slice_add_fusion.7), channel_id=1, source_target_pairs={{0,16},{2,18},{4,20},{6,22},{8,24},{10,26},{12,28},{14,30},{16,0},... | collective-permute-start | bytes 884744 | tf_op jit(solution)/shard_map/ppermute | solution.py:48
  (72 other events, 683.4 us)
